TPU v7x, 32 devices: a whole 2x2x4 slice. The times are simulated.
32 devices in a mesh: groups: 2 (over y), owner: 4 (over z), sub: 2 (over x), pair: 2 (over core).
Axes of the slice: x: 2, y: 2, z: 4, core: 2. Of those that a mesh axis runs over, the one named last changes fastest.
Arguments:
- embeddings: float32 [16, 2, 128, 1152], P(('groups', 'owner', 'sub'), 'pair'), parts along dimension 0, may hold values from -12 to 12
- moves: int32 [2, 16, 2, 128], P(None, ('groups', 'owner', 'sub'), 'pair'), parts along dimension 1, may hold values from -1 to 7, as said below
Outputs:
- curated: float32 [16, 2, 128, 1152], P(('groups', 'owner', 'sub'), 'pair'), parts along dimension 0
There are 2 independent parts, one for each index of `groups`. A program takes and returns all parts, laid end to end along the dimension named above; each array names one. Nothing has to cross between parts.
Inputs may be any that keep to these rules, and one draw needn't show every extreme that they name: moves[m, c, p, s] is the cluster to which the row in slot s of device (c, p) goes after pass m + 1, or -1 for an empty slot; the row stays on pair index p. A device's live slots come first. In one list at most 16 live rows of one device go to one cluster, and some device sends 16 to every cluster; some device holds 128 live rows and some device receives 128, in every list. The live slots of a device in list m + 1 number exactly the rows it receives from list m.
All inputs are finite; a program needn't handle non-finite values.
Results may differ from a plain program's by a relative error of at most 0.002.
Values may be sent and summed in bfloat16 or wider, within the bound.
No kernel may reach another device: no remote copies, remote signals or barrier semaphores. Data moves between devices by JAX's collectives and lax.ppermute only.
A program may use at most 64 MiB of HBM per device.

v0:
```python
import jax
import jax.numpy as jnp
from jax import lax
from jax.sharding import PartitionSpec as P

PASSES = 3


epsilon = 1e-06
sharpness = 6.0


def unit_rows(values):
    return values / jnp.sqrt(jnp.sum(values * values, axis=1, keepdims=True) + epsilon)


def shift_pass(state, live_mask):
    marks = live_mask.astype(jnp.bfloat16)
    key_rows = lax.all_gather(state, "pair", axis=0, tiled=True)
    key_marks = lax.all_gather(marks, "pair", axis=0, tiled=True)
    scores = lax.dot_general(
        state, key_rows, (((1,), (1,)), ((), ())), preferred_element_type=jnp.float32
    )
    weights = jnp.where(key_marks[None, :] > 0, jnp.exp(sharpness * (scores - 1.0)), 0.0).astype(
        jnp.bfloat16
    )
    numer = jnp.dot(weights, key_rows, preferred_element_type=jnp.float32)
    denom = jnp.sum(weights.astype(jnp.float32), axis=1)
    numer, denom = (numer, denom)
    shifted = numer / jnp.where(live_mask, denom, 1.0)[:, None]
    return jnp.where(live_mask[:, None], unit_rows(shifted), 0.0)


def migrate(state, targets):
    rows_cap = state.shape[0]
    width = state.shape[1]
    owners = lax.axis_size("owner")
    clusters = owners * lax.axis_size("sub")
    most = rows_cap // clusters
    cluster_ids = jnp.arange(clusters, dtype=jnp.int32)
    slot_ids = jnp.arange(rows_cap, dtype=jnp.int32)
    onehot = (targets[:, None] == cluster_ids[None, :]).astype(jnp.int32)
    ranks = jnp.sum(jnp.cumsum(onehot, axis=0) * onehot, axis=1) - 1
    send_counts = jnp.sum(onehot, axis=0)
    bucket = jnp.where(targets >= 0, targets * most + ranks, -1)
    positions = jnp.arange(clusters * most, dtype=jnp.int32)
    matches = bucket[None, :] == positions[:, None]
    source_slot = jnp.sum(jnp.where(matches, slot_ids[None, :], 0), axis=1)
    filled = jnp.any(matches, axis=1)
    outgoing = jnp.where(filled[:, None], jnp.take(state, source_slot, axis=0), 0.0)
    arrived, counts_in = (
        lax.all_to_all(
            outgoing.reshape(clusters, most, width),
            ("owner", "sub"),
            split_axis=0,
            concat_axis=0,
            tiled=True,
        ),
        lax.all_to_all(send_counts, ("owner", "sub"), split_axis=0, concat_axis=0, tiled=True),
    )
    arrived = arrived.reshape(clusters * most, width)
    ends = jnp.cumsum(counts_in)
    starts = ends - counts_in
    source_block = jnp.sum((ends[None, :] <= slot_ids[:, None]).astype(jnp.int32), axis=1)
    block_start = jnp.sum(
        jnp.where(source_block[:, None] == cluster_ids[None, :], starts[None, :], 0), axis=1
    )
    flat_index = jnp.minimum(source_block * most + slot_ids - block_start, clusters * most - 1)
    new_mask = slot_ids < ends[-1]
    new_state = jnp.where(new_mask[:, None], jnp.take(arrived, flat_index, axis=0), 0.0)
    return (new_state, new_mask)


def body(embeddings, moves):
    targets = moves[:, 0, 0, :]
    live_mask = targets[0] >= 0
    state = jnp.where(live_mask[:, None], unit_rows(embeddings[0, 0]), 0.0).astype(jnp.bfloat16)
    result = jnp.zeros(embeddings.shape[2:], jnp.float32)
    for number in range(PASSES):
        result = shift_pass(state, live_mask)
        if number + 1 < PASSES:
            state, live_mask = migrate(result.astype(jnp.bfloat16), targets[number])
    return result[None, None]


def solution(mesh):
    placed = (
        P(("groups", "owner", "sub"), "pair", None, None),
        P(None, ("groups", "owner", "sub"), "pair", None),
    )
    return jax.shard_map(
        body,
        mesh=mesh,
        in_specs=placed,
        out_specs=P(("groups", "owner", "sub"), "pair", None, None),
        check_vma=False,
    )
```

profile of v0, /device:TPU:0, one launch (start us, length us, event | category | flops | bytes accessed | tf_op | source)
XLA Modules:
  0.0 73.5 jit_solution(1787481121219910143)
XLA Ops:
  0.0 0.7 %slice_bitcast_fusion.1 = (s32[128]{0:T(128)S(1)}, s32[128]{0:T(128)S(1)}) fusion(s32[2,1,1,128]{3,2,1,0:T(1,128)} %param.5), kind=kLoop, calls=%fused_computation.85 | loop fusion | bytes 2048 | tf_op jit(solution)/shard_map/eq | solution.py:42
  1.0 0.2 fusion.20
  1.2 0.7 copy.8
  1.9 7.3 %all-to-all-start.1 = ((s32[8,1,1]{2,1,0:T(1,128)}), s32[8,1,1]{2,1,0:T(1,128)S(1)}, u32[]{:S(2)}, u32[]{:S(2)}) async-start(s32[8,1,1]{2,1,0:T(1,128)} %copy.8), calls=%async_computation.1 | async-start | bytes 8192 | tf_op jit(solution)/shard_map/all_to_all | solution.py:59
  9.2 0.7 convert_bitcast_fusion
  10.2 0.7 compare_select_fusion.4
  11.3 1.2 %fusion.12 = f32[128]{0:T(128)S(1)} fusion(f32[1,1,128,1152]{3,2,1,0:T(8,128)} %param.4), kind=kLoop, calls=%fused_computation.21 | loop fusion | flops 294784 | bytes 590336 | tf_op jit(solution)/shard_map/reduce_sum | solution.py:14
  12.7 2.2 %all_gather.21 = bf16[256,1152]{1,0:T(8,128)(2,1)S(1)} all-gather(bf16[128,1152]{1,0:T(8,128)(2,1)S(1)} %fusion.14), channel_id=1, replica_groups=mesh['groups'=2,'owner'=4,'sub'=2,'pair'=2] {'pair'}, dimensions={0}, use_global_device_ids=true | all-gather | bytes 884736 | tf_op jit(solution)/shard_map/all_gather | solution.py:19
  14.9 1.8 %all-gather.2 = bf16[2,1,128]{2,1,0:T(2,128)(2,1)S(1)} all-gather(bf16[1,1,128]{2,1,0:T(2,128)(2,1)S(1)} %get-tuple-element.18), channel_id=1, replica_groups=mesh['groups'=2,'owner'=4,'sub'=2,'pair'=2] {'pair'}, dimensions={0}, use_global_device_ids=true | all-gather | bytes 768 | tf_op jit(solution)/shard_map/all_gather | solution.py:20
  16.7 0.4 convert_reduce_fusion.2
  17.2 0.7 copy-done.1
  17.9 0.3 multiply_reduce_fusion.2
  18.4 0.9 %gather_fusion = bf16[128,1152]{1,0:T(8,128)(2,1)S(1)} fusion(bf16[128,1152]{1,0:T(8,128)(2,1)S(1)} %select_convert_fusion.1, s32[1024]{0:T(1024)S(1)} %pad_clamp_fusion.3), kind=kCustom, calls=%fused_computation.clone | custom fusion | bytes 590336 | tf_op jit(solution)/shard_map/jit(_take)/gather | solution.py:50
  19.3 0.8 %select_select_fusion.3 = bf16[128,1152]{1,0:T(8,128)(2,1)} fusion(bf16[128,1152]{1,0:T(8,128)(2,1)S(1)} %gather_fusion, pred[128]{0:T(512)(128)(4,1)S(1)} %compare_and_fusion.3, pred[128]{0:T(512)(128)(4,1)S(1)} %fusion.15), kind=kLoop, calls=%fused_computation.33 | loop fusion | flops 294912 | bytes 590080 | tf_op jit(solution)/shard_map/jit(_where)/select_n | solution.py:50
  20.1 0.7 copy.7
  20.8 6.0 %all-to-all-start = ((s32[8,1,1]{2,1,0:T(1,128)}), s32[8,1,1]{2,1,0:T(1,128)S(1)}, u32[]{:S(2)}, u32[]{:S(2)}) async-start(s32[8,1,1]{2,1,0:T(1,128)} %copy.7), calls=%async_computation | async-start | bytes 8192 | tf_op jit(solution)/shard_map/all_to_all | solution.py:59
  26.8 0.2 reduce.3
  27.0 0.2 reduce-window.9
  27.2 0.6 slice.20
  28.1 0.6 convert_bitcast_fusion.1
  28.7 1.8 %all-gather.1 = bf16[2,1,128]{2,1,0:T(2,128)(2,1)S(1)} all-gather(bf16[1,1,128]{2,1,0:T(2,128)(2,1)S(1)} %convert_bitcast_fusion.1), channel_id=1, replica_groups=mesh['groups'=2,'owner'=4,'sub'=2,'pair'=2] {'pair'}, dimensions={0}, use_global_device_ids=true | all-gather | bytes 768 | tf_op jit(solution)/shard_map/all_gather | solution.py:20
  30.5 2.8 %all-to-all-done = s32[8,1,1]{2,1,0:T(1,128)S(1)} async-done(((s32[8,1,1]{2,1,0:T(1,128)}), s32[8,1,1]{2,1,0:T(1,128)S(1)}, u32[]{:S(2)}, u32[]{:S(2)}) %all-to-all-start) | async-done | bytes 64 | tf_op jit(solution)/shard_map/all_to_all | solution.py:59
  33.3 3.4 %all-to-all-start.2 = ((bf16[8,16,1152]{2,1,0:T(8,128)(2,1)}), bf16[8,16,1152]{2,1,0:T(8,128)(2,1)S(1)}, u32[]{:S(2)}, u32[]{:S(2)}) async-start(bf16[8,16,1152]{2,1,0:T(8,128)(2,1)} %bitcast.12), calls=%async_computation.2 | async-start | bytes 589824 | tf_op jit(solution)/shard_map/all_to_all | solution.py:52
  36.7 0.2 reduce
  37.0 0.2 reduce-window.6
  37.2 0.7 slice.18
  37.8 0.7 convert_bitcast_fusion.2
  38.5 1.8 %all-gather = bf16[2,1,128]{2,1,0:T(2,128)(2,1)S(1)} all-gather(bf16[1,1,128]{2,1,0:T(2,128)(2,1)S(1)} %convert_bitcast_fusion.2), channel_id=1, replica_groups=mesh['groups'=2,'owner'=4,'sub'=2,'pair'=2] {'pair'}, dimensions={0}, use_global_device_ids=true | all-gather | bytes 768 | tf_op jit(solution)/shard_map/all_gather | solution.py:20
  40.3 0.6 iota_compare_fusion.8
  41.2 5.3 %all-to-all-done.2 = bf16[8,16,1152]{2,1,0:T(8,128)(2,1)S(1)} async-done(((bf16[8,16,1152]{2,1,0:T(8,128)(2,1)}), bf16[8,16,1152]{2,1,0:T(8,128)(2,1)S(1)}, u32[]{:S(2)}, u32[]{:S(2)}) %all-to-all-start.2) | async-done | bytes 294944 | tf_op jit(solution)/shard_map/all_to_all | solution.py:52
  46.4 0.9 %gather_fusion.1 = bf16[128,1152]{1,0:T(8,128)(2,1)S(1)} fusion(bf16[128,1152]{1,0:T(8,128)(2,1)S(1)} %bitcast.62, s32[1024]{0:T(1024)S(1)} %pad_clamp_fusion.2), kind=kCustom, calls=%fused_computation.1.clone | custom fusion | bytes 590336 | tf_op jit(solution)/shard_map/jit(_take)/gather | solution.py:70
  47.5 2.2 %all_gather.22 = bf16[256,1152]{1,0:T(8,128)(2,1)S(1)} all-gather(bf16[128,1152]{1,0:T(8,128)(2,1)S(1)} %select_select_fusion.2), channel_id=1, replica_groups=mesh['groups'=2,'owner'=4,'sub'=2,'pair'=2] {'pair'}, dimensions={0}, use_global_device_ids=true | all-gather | bytes 884736 | tf_op jit(solution)/shard_map/all_gather | solution.py:19
  49.7 0.4 convert_reduce_fusion.1
  50.1 0.6 broadcast_select_fusion.1
  50.7 0.3 multiply_reduce_fusion.1
  51.1 0.6 sqrt_multiply_fusion.1
  51.8 0.9 %gather_fusion.2 = bf16[128,1152]{1,0:T(8,128)(2,1)S(1)} fusion(bf16[128,1152]{1,0:T(8,128)(2,1)S(1)} %select_convert_fusion, s32[1024]{0:T(1024)S(1)} %pad_clamp_fusion.1), kind=kCustom, calls=%fused_computation.2.clone | custom fusion | bytes 590336 | tf_op jit(solution)/shard_map/jit(_take)/gather | solution.py:50
  52.7 0.8 %select_select_fusion.1 = bf16[128,1152]{1,0:T(8,128)(2,1)} fusion(bf16[128,1152]{1,0:T(8,128)(2,1)S(1)} %gather_fusion.2, pred[128]{0:T(512)(128)(4,1)S(1)} %compare_and_fusion.1, pred[128]{0:T(512)(128)(4,1)S(1)} %fusion.17), kind=kLoop, calls=%fused_computation.31 | loop fusion | flops 294912 | bytes 590080 | tf_op jit(solution)/shard_map/jit(_where)/select_n | solution.py:50
  53.5 3.6 %all-to-all-start.3 = ((bf16[8,16,1152]{2,1,0:T(8,128)(2,1)}), bf16[8,16,1152]{2,1,0:T(8,128)(2,1)S(1)}, u32[]{:S(2)}, u32[]{:S(2)}) async-start(bf16[8,16,1152]{2,1,0:T(8,128)(2,1)} %bitcast.14), calls=%async_computation.3 | async-start | bytes 589824 | tf_op jit(solution)/shard_map/all_to_all | solution.py:52
  57.2 0.7 iota_compare_fusion.9
  57.9 9.1 %all-to-all-done.3 = bf16[8,16,1152]{2,1,0:T(8,128)(2,1)S(1)} async-done(((bf16[8,16,1152]{2,1,0:T(8,128)(2,1)}), bf16[8,16,1152]{2,1,0:T(8,128)(2,1)S(1)}, u32[]{:S(2)}, u32[]{:S(2)}) %all-to-all-start.3) | async-done | bytes 294944 | tf_op jit(solution)/shard_map/all_to_all | solution.py:52
  67.0 0.9 %gather_fusion.3 = bf16[128,1152]{1,0:T(8,128)(2,1)S(1)} fusion(bf16[128,1152]{1,0:T(8,128)(2,1)S(1)} %bitcast.63, s32[1024]{0:T(1024)S(1)} %pad_clamp_fusion), kind=kCustom, calls=%fused_computation.3.clone | custom fusion | bytes 590336 | tf_op jit(solution)/shard_map/jit(_take)/gather | solution.py:70
  68.1 2.2 %all_gather.23 = bf16[256,1152]{1,0:T(8,128)(2,1)S(1)} all-gather(bf16[128,1152]{1,0:T(8,128)(2,1)S(1)} %select_select_fusion), channel_id=1, replica_groups=mesh['groups'=2,'owner'=4,'sub'=2,'pair'=2] {'pair'}, dimensions={0}, use_global_device_ids=true | all-gather | bytes 884736 | tf_op jit(solution)/shard_map/all_gather | solution.py:19
  70.3 0.4 convert_reduce_fusion
  70.7 0.7 broadcast_select_fusion
  71.5 0.3 multiply_reduce_fusion
  71.8 0.7 sqrt_multiply_fusion
  72.5 0.9 %select_bitcast_fusion = f32[1,1,128,1152]{3,2,1,0:T(8,128)} fusion(f32[128,1152]{1,0:T(8,128)S(1)} %get-tuple-element.31, f32[128]{0:T(128)S(1)} %sqrt_multiply_fusion, pred[128]{0:T(512)(128)(4,1)S(1)} %iota_compare_fusion.9), kind=kLoop, calls=%fused_computation.24 | loop fusion | flops 294912 | bytes 1180288 | tf_op jit(solution)/shard_map/broadcast_in_dim | solution.py:83
  (39 shorter events, 2.4 us)
Async XLA Ops:
  0.0 12.5 %copy-start = (f32[1,1,128,1152]{3,2,1,0:T(8,128)S(1)}, f32[1,1,128,1152]{3,2,1,0:T(8,128)}, u32[]{:S(2)}) copy-start(f32[1,1,128,1152]{3,2,1,0:T(8,128)} %param.4) | copy-start | bytes 1769476
  1.9 18.9 %all-to-all-start.1 = ((s32[8,1,1]{2,1,0:T(1,128)}), s32[8,1,1]{2,1,0:T(1,128)S(1)}, u32[]{:S(2)}, u32[]{:S(2)}) async-start(s32[8,1,1]{2,1,0:T(1,128)} %copy.8), calls=%async_computation.1 | async-start | bytes 8192 | tf_op jit(solution)/shard_map/all_to_all | solution.py:59
  17.2 0.7 copy-start.1
  20.8 12.5 %all-to-all-start = ((s32[8,1,1]{2,1,0:T(1,128)}), s32[8,1,1]{2,1,0:T(1,128)S(1)}, u32[]{:S(2)}, u32[]{:S(2)}) async-start(s32[8,1,1]{2,1,0:T(1,128)} %copy.7), calls=%async_computation | async-start | bytes 8192 | tf_op jit(solution)/shard_map/all_to_all | solution.py:59
  33.3 13.1 %all-to-all-start.2 = ((bf16[8,16,1152]{2,1,0:T(8,128)(2,1)}), bf16[8,16,1152]{2,1,0:T(8,128)(2,1)S(1)}, u32[]{:S(2)}, u32[]{:S(2)}) async-start(bf16[8,16,1152]{2,1,0:T(8,128)(2,1)} %bitcast.12), calls=%async_computation.2 | async-start | bytes 589824 | tf_op jit(solution)/shard_map/all_to_all | solution.py:52
  53.5 13.5 %all-to-all-start.3 = ((bf16[8,16,1152]{2,1,0:T(8,128)(2,1)}), bf16[8,16,1152]{2,1,0:T(8,128)(2,1)S(1)}, u32[]{:S(2)}, u32[]{:S(2)}) async-start(bf16[8,16,1152]{2,1,0:T(8,128)(2,1)} %bitcast.14), calls=%async_computation.3 | async-start | bytes 589824 | tf_op jit(solution)/shard_map/all_to_all | solution.py:52
where the time goes:
time: 74.1 us; the launch traced here: 73.5 us
  starting transfers between devices  20.3 us (27%)
  waiting for transfers between devices  17.2 us (23%)
  other arithmetic  13.6 us (18%)
  blocking collectives  12.1 us (16%)
  local copies, waits for them, and re-layouts  7.63 us (10%)
  matrix products  2.32 us (3%)
    all_to_all x2, waiting for transfers between devices, migrate(): lax.all_to_all(outgoing.reshape(clusters, most, width), ('owner', 'sub'),...  14.4 us
    all_to_all x2, starting transfers between devices, migrate(): lax.all_to_all(send_counts, ('owner', 'sub'), split_axis=0, concat_axis=0...  13.3 us
    all_to_all x2, starting transfers between devices, migrate(): lax.all_to_all(outgoing.reshape(clusters, most, width), ('owner', 'sub'),...  7.06 us
    all_gather x3, blocking collectives, shift_pass(): key_rows = lax.all_gather(state, 'pair', axis=0, tiled=True)  6.69 us
    all_gather x3, blocking collectives, shift_pass(): key_marks = lax.all_gather(marks, 'pair', axis=0, tiled=True)  5.41 us
    all_to_all x2, waiting for transfers between devices, migrate(): lax.all_to_all(send_counts, ('owner', 'sub'), split_axis=0, concat_axis=0...  2.79 us
    unnamed x3, other arithmetic  1.91 us
    gather x2, local copies, waits for them, and re-layouts, migrate(): jnp.take(arrived, flat_index, axis=0)  1.81 us
  transfers between devices with their start and end apart: 4, of which 3 were waited for; matrix products, arithmetic and copies ran while one was open for 16% of the time, Pallas kernels for 0%

commit v1 on v0

v1 whole, which is shorter than its diff:
```python
import jax
import jax.numpy as jnp
from jax import lax
from jax.experimental import pallas as pl
from jax.experimental.pallas import tpu as pltpu
from jax.sharding import PartitionSpec as P

PASSES = 3
LANES = 128
MARK = 2.0

epsilon = 1e-06
sharpness = 6.0

f32 = jnp.float32
bf16 = jnp.bfloat16


def mark_empty(block, filled):
    lane = lax.broadcasted_iota(jnp.int32, block.shape, 1)
    return jnp.where((lane == 0) & (filled < 0.5), MARK, block)


def state_kernel(emb_ref, moves_ref, out_ref):
    rows = emb_ref.shape[0]
    values = emb_ref[...]
    count = jnp.sum((moves_ref[0:1, :] >= 0).astype(f32), axis=1, keepdims=True)
    slot = lax.broadcasted_iota(jnp.int32, (rows, LANES), 0).astype(f32)
    live = (slot < count).astype(f32)
    total = jnp.sum(values * values, axis=1, keepdims=True)
    unit = values * lax.rsqrt(total + epsilon)
    unit = jnp.where(live[:, 0:1] > 0.5, unit, 0.0)
    out_ref[:, LANES:] = unit[:, LANES:].astype(bf16)
    out_ref[:, :LANES] = mark_empty(unit[:, :LANES], live).astype(bf16)


def places_kernel(clusters, most, moves_ref, out_ref):
    lists, rows = moves_ref.shape
    before = lax.broadcasted_iota(jnp.int32, (rows, rows), 0) < lax.broadcasted_iota(
        jnp.int32, (rows, rows), 1
    )
    before = before.astype(bf16)
    cluster = lax.broadcasted_iota(jnp.int32, (clusters, rows), 0)
    for number in range(lists):
        targets = moves_ref[number : number + 1, :]
        onehot = (cluster == targets).astype(f32)
        earlier = jnp.dot(onehot.astype(bf16), before, preferred_element_type=f32)
        rank = jnp.sum(onehot * earlier, axis=0, keepdims=True)
        place = targets * most + rank.astype(jnp.int32)
        out_ref[number : number + 1, :] = jnp.where(targets >= 0, place, -1)


def pass_kernel(compact, last, number, own_ref, peer_ref, places_ref, out_ref):
    rows, width = own_ref.shape

    def cleaned(ref):
        head = ref[:, :LANES].astype(f32)
        live = (head[:, 0:1] < 1.5).astype(f32)
        live = jnp.broadcast_to(live, (rows, LANES))
        head = jnp.where(live > 0.5, head, 0.0)
        return jnp.concatenate(
            [head.astype(bf16), ref[:, LANES:], live.astype(bf16)], axis=1
        ), live

    own, own_live = cleaned(own_ref)
    peer, _ = cleaned(peer_ref)
    keys = jnp.concatenate([own, peer], axis=0)
    if compact:
        row = lax.broadcasted_iota(jnp.int32, (rows, rows), 0)
        col = lax.broadcasted_iota(jnp.int32, (rows, rows), 1)
        dest = jnp.dot(
            (col < row).astype(bf16), own_live.astype(bf16), preferred_element_type=f32
        )
        slots = lax.broadcasted_iota(jnp.int32, (rows, LANES), 1).astype(f32)
        select = ((dest == slots) & (own_live > 0.5)).astype(bf16)
        query = lax.dot_general(
            select, own, (((0,), (0,)), ((), ())), preferred_element_type=f32
        )
        query_live = query[:, width:]
        query = query[:, :width].astype(bf16)
    else:
        query_live = own_live
        query = own[:, :width]
    scores = lax.dot_general(
        query, keys[:, :width], (((1,), (1,)), ((), ())), preferred_element_type=f32
    )
    weights = jnp.exp(sharpness * (scores - 1.0)).astype(bf16)
    sums = jnp.dot(weights, keys, preferred_element_type=f32)
    numer = sums[:, :width]
    inverse = 1.0 / sums[:, width : width + 1]
    total = jnp.sum(numer * numer, axis=1, keepdims=True)
    scale = inverse * lax.rsqrt(total * (inverse * inverse) + epsilon)
    unit = jnp.where(query_live[:, 0:1] > 0.5, numer * scale, 0.0)
    if last:
        out_ref[...] = unit
        return
    place = places_ref[number : number + 1, :]
    wanted = lax.broadcasted_iota(jnp.int32, (rows, rows), 0)
    choose = (wanted == place).astype(bf16)
    filled = jnp.sum(choose.astype(f32), axis=1, keepdims=True)
    outgoing = jnp.dot(choose, unit.astype(bf16), preferred_element_type=f32)
    out_ref[:, LANES:] = outgoing[:, LANES:].astype(bf16)
    out_ref[:, :LANES] = mark_empty(outgoing[:, :LANES], filled).astype(bf16)


def call(kernel, out, *args):
    spec = pl.BlockSpec(memory_space=pltpu.VMEM)
    return pl.pallas_call(
        kernel, out_shape=out, in_specs=[spec] * len(args), out_specs=spec
    )(*args)


def swap_pair(values):
    return lax.ppermute(values, "pair", [(0, 1), (1, 0)])


def body(embeddings, moves):
    rows, width = embeddings.shape[2:]
    clusters = lax.axis_size("owner") * lax.axis_size("sub")
    most = rows // clusters
    targets = moves[:, 0, 0, :]
    state = call(
        state_kernel, jax.ShapeDtypeStruct((rows, width), bf16), embeddings[0, 0], targets
    )
    places = call(
        lambda *refs: places_kernel(clusters, most, *refs),
        jax.ShapeDtypeStruct(targets.shape, jnp.int32),
        targets,
    )
    for number in range(PASSES):
        last = number + 1 == PASSES
        peer = swap_pair(state)
        result = call(
            lambda *refs: pass_kernel(number > 0, last, number, *refs),
            jax.ShapeDtypeStruct((rows, width), f32 if last else bf16),
            state,
            peer,
            places,
        )
        if not last:
            state = lax.all_to_all(
                result.reshape(clusters, most, width),
                ("owner", "sub"),
                split_axis=0,
                concat_axis=0,
                tiled=True,
            ).reshape(rows, width)
    return result[None, None]


def solution(mesh):
    placed = (
        P(("groups", "owner", "sub"), "pair", None, None),
        P(None, ("groups", "owner", "sub"), "pair", None),
    )
    return jax.shard_map(
        body,
        mesh=mesh,
        in_specs=placed,
        out_specs=P(("groups", "owner", "sub"), "pair", None, None),
        check_vma=False,
    )
```

time: 74.1 us -> 50.9 us (0.69)
  blocking collectives: 12.1 us -> 32 us
  starting transfers between devices: 20.3 us -> 0.5 us
  waiting for transfers between devices: 17.2 us -> 3.21 us
  other arithmetic: 13.6 us -> 0 us
  Pallas kernels: 0 us -> 12.6 us
  local copies, waits for them, and re-layouts: 7.63 us -> 2.13 us
  matrix products: 2.32 us -> 0 us
    all_to_all x0 -> x2, blocking collectives: none -> 32 us  [body(): lax.all_to_all(result.reshape(clusters, most, width), ('owner', 'sub'), s...]
    all_to_all x4 -> x0, starting transfers between devices: 20.3 us -> none  [the longest x2 13.3 us: migrate(): lax.all_to_all(send_counts, ('owner', 'sub'), split_axis=0, concat_axis=0...]
    all_to_all x4 -> x0, waiting for transfers between devices: 17.2 us -> none  [the longest x2 14.4 us: migrate(): lax.all_to_all(outgoing.reshape(clusters, most, width), ('owner', 'sub'),...]
    pallas_call x0 -> x5, Pallas kernels: none -> 12.6 us  [call(): pl.pallas_call(kernel, out_shape=out, in_specs=[spec] * len(args), out_sp...]
    all_gather x6 -> x0, blocking collectives: 12.1 us -> none  [the longest x3 6.69 us: shift_pass(): key_rows = lax.all_gather(state, 'pair', axis=0, tiled=True)]
    select_n x10 -> x0, other arithmetic: 3.91 us -> none  [the longest x2 1.69 us: migrate(): jnp.where(filled[:, None], jnp.take(state, source_slot, axis=0), 0.0)]
    gather x4 -> x0, local copies, waits for them, and re-layouts: 3.61 us -> none  [the longest x2 1.81 us: migrate(): jnp.take(arrived, flat_index, axis=0)]
    ppermute x0 -> x3, waiting for transfers between devices: none -> 3.21 us  [swap_pair(): return lax.ppermute(values, 'pair', [(0, 1), (1, 0)])]
  transfers between devices with their start and end apart: 4 -> 3, of which waited for: 3 -> 3; matrix products, arithmetic and copies ran while one was open for 16% -> 0% of each run, Pallas kernels for 0% -> 3%
where the time goes in v1:
time: 50.9 us; the launch traced here: 50.5 us
  blocking collectives  32 us (63%)
  Pallas kernels  12.6 us (25%)
  waiting for transfers between devices  3.21 us (6%)
  local copies, waits for them, and re-layouts  2.13 us (4%)
    all_to_all x2, blocking collectives, body(): lax.all_to_all(result.reshape(clusters, most, width), ('owner', 'sub'), s...  32 us
    pallas_call x5, Pallas kernels, call(): pl.pallas_call(kernel, out_shape=out, in_specs=[spec] * len(args), out_sp...  12.6 us
    ppermute x3, waiting for transfers between devices, swap_pair(): return lax.ppermute(values, 'pair', [(0, 1), (1, 0)])  3.21 us
    unnamed x10, local copies, waits for them, and re-layouts  2.13 us
  transfers between devices with their start and end apart: 3, of which 3 were waited for; matrix products, arithmetic and copies ran while one was open for 0% of the time, Pallas kernels for 3%

profile of v1, /device:TPU:0, one launch (start us, length us, event | category | flops | bytes accessed | tf_op | source)
XLA Modules:
  0.0 50.5 jit_solution(14071167505243977619)
XLA Ops:
  0.0 2.0 %shard_map.28.refs_0_ = bf16[128,1152]{1,0:T(8,128)(2,1)} custom-call(f32[128,1152]{1,0:T(8,128)} %bitcast.13, s32[2,128]{1,0:T(2,128)} %bitcast.14), custom_call_target="tpu_custom_call" | custom-call | tf_op jit(solution)/shard_map/pallas_call | solution.py:108
  2.0 0.5 collective-permute-start
  2.5 1.4 %shard_map.29.refs_2_ = s32[2,128]{1,0:T(2,128)} custom-call(s32[2,128]{1,0:T(2,128)} %bitcast.15), custom_call_target="tpu_custom_call" | custom-call | tf_op jit(solution)/shard_map/pallas_call | solution.py:108
  3.8 0.1 collective-permute-done.refs_1_
  3.9 0.0 copy-start.2
  3.9 0.7 %copy-done.2 = bf16[128,1152]{1,0:T(8,128)(2,1)} copy-done((bf16[128,1152]{1,0:T(8,128)(2,1)}, bf16[128,1152]{1,0:T(8,128)(2,1)S(1)}, u32[]{:S(2)}) %copy-start.2) | copy-done | bytes 294936
  4.6 3.0 %shard_map.30 = bf16[128,1152]{1,0:T(8,128)(2,1)} custom-call(bf16[128,1152]{1,0:T(8,128)(2,1)} %shard_map.28.refs_0_, bf16[128,1152]{1,0:T(8,128)(2,1)} %copy-done.2, s32[2,128]{1,0:T(2,128)} %shard_map.29.refs_2_), custom_call_target="tpu_custom_call" | custom-call | tf_op jit(solution)/shard_map/pallas_call | solution.py:108
  7.6 17.8 %all_to_all.10 = bf16[8,16,1152]{2,1,0:T(8,128)(2,1)S(1)} all-to-all(bf16[8,16,1152]{2,1,0:T(8,128)(2,1)} %bitcast.11), channel_id=1, replica_groups=mesh['groups'=2,'owner'=4,'sub'=2,'pair'=2] {'owner','sub'}, dimensions={0} | all-to-all | bytes 589824 | tf_op jit(solution)/shard_map/all_to_all | solution.py:141
  25.4 0.0 copy-start.1
  25.4 0.0 collective-permute-start.1
  25.4 1.6 %collective-permute-done.1.refs_1_ = bf16[128,1152]{1,0:T(8,128)(2,1)S(1)} collective-permute-done((bf16[128,1152]{1,0:T(8,128)(2,1)S(1)}, bf16[128,1152]{1,0:T(8,128)(2,1)S(1)}, u32[]{:S(2)}, u32[]{:S(2)}) %collective-permute-start.1) | collective-permute-done | bytes 294944 | tf_op jit(solution)/shard_map/ppermute | solution.py:114
  27.0 0.0 copy-done.1
  27.0 0.0 copy-start.4
  27.0 0.7 %copy-done.4 = bf16[128,1152]{1,0:T(8,128)(2,1)} copy-done((bf16[128,1152]{1,0:T(8,128)(2,1)}, bf16[128,1152]{1,0:T(8,128)(2,1)S(1)}, u32[]{:S(2)}) %copy-start.4) | copy-done | bytes 294936
  27.7 3.2 %shard_map.31 = bf16[128,1152]{1,0:T(8,128)(2,1)} custom-call(bf16[128,1152]{1,0:T(8,128)(2,1)} %bitcast.10, bf16[128,1152]{1,0:T(8,128)(2,1)} %copy-done.4, s32[2,128]{1,0:T(2,128)} %shard_map.29.refs_2_), custom_call_target="tpu_custom_call" | custom-call | tf_op jit(solution)/shard_map/pallas_call | solution.py:108
  30.9 14.2 %all_to_all.11 = bf16[8,16,1152]{2,1,0:T(8,128)(2,1)S(1)} all-to-all(bf16[8,16,1152]{2,1,0:T(8,128)(2,1)} %bitcast.12), channel_id=1, replica_groups=mesh['groups'=2,'owner'=4,'sub'=2,'pair'=2] {'owner','sub'}, dimensions={0} | all-to-all | bytes 589824 | tf_op jit(solution)/shard_map/all_to_all | solution.py:141
  45.2 0.0 copy-start
  45.2 0.0 collective-permute-start.2
  45.2 1.6 %collective-permute-done.2.refs_1_ = bf16[128,1152]{1,0:T(8,128)(2,1)S(1)} collective-permute-done((bf16[128,1152]{1,0:T(8,128)(2,1)S(1)}, bf16[128,1152]{1,0:T(8,128)(2,1)S(1)}, u32[]{:S(2)}, u32[]{:S(2)}) %collective-permute-start.2) | collective-permute-done | bytes 294944 | tf_op jit(solution)/shard_map/ppermute | solution.py:114
  46.7 0.0 copy-done
  46.7 0.0 copy-start.3
  46.7 0.7 %copy-done.3 = bf16[128,1152]{1,0:T(8,128)(2,1)} copy-done((bf16[128,1152]{1,0:T(8,128)(2,1)}, bf16[128,1152]{1,0:T(8,128)(2,1)S(1)}, u32[]{:S(2)}) %copy-start.3) | copy-done | bytes 294936
  47.4 3.0 %shard_map.32 = f32[128,1152]{1,0:T(8,128)} custom-call(bf16[128,1152]{1,0:T(8,128)(2,1)} %bitcast.8, bf16[128,1152]{1,0:T(8,128)(2,1)} %copy-done.3, s32[2,128]{1,0:T(2,128)} %shard_map.29.refs_2_), custom_call_target="tpu_custom_call" | custom-call | tf_op jit(solution)/shard_map/pallas_call | solution.py:108
Async XLA Ops:
  2.0 1.9 %collective-permute-start = (bf16[128,1152]{1,0:T(8,128)(2,1)}, bf16[128,1152]{1,0:T(8,128)(2,1)S(1)}, u32[]{:S(2)}, u32[]{:S(2)}) collective-permute-start(bf16[128,1152]{1,0:T(8,128)(2,1)} %shard_map.28.refs_0_), channel_id=1, source_target_pairs={{0,1},{1,0},{2,3},{3,2},{4,5},{5,4},{6,7},{7,6},{8,9},{9,8},{10,11... | collective-permute-start | bytes 884744 | tf_op jit(solution)/shard_map/ppermute | solution.py:114
  3.9 0.7 %copy-start.2 = (bf16[128,1152]{1,0:T(8,128)(2,1)}, bf16[128,1152]{1,0:T(8,128)(2,1)S(1)}, u32[]{:S(2)}) copy-start(bf16[128,1152]{1,0:T(8,128)(2,1)S(1)} %collective-permute-done.refs_1_) | copy-start | bytes 884740
  25.4 1.6 %copy-start.1 = (bf16[8,16,1152]{2,1,0:T(8,128)(2,1)}, bf16[8,16,1152]{2,1,0:T(8,128)(2,1)S(1)}, u32[]{:S(2)}) copy-start(bf16[8,16,1152]{2,1,0:T(8,128)(2,1)S(1)} %all_to_all.10) | copy-start | bytes 884740
  25.4 1.6 %collective-permute-start.1 = (bf16[128,1152]{1,0:T(8,128)(2,1)S(1)}, bf16[128,1152]{1,0:T(8,128)(2,1)S(1)}, u32[]{:S(2)}, u32[]{:S(2)}) collective-permute-start(bf16[128,1152]{1,0:T(8,128)(2,1)S(1)} %bitcast.9), channel_id=1, source_target_pairs={{0,1},{1,0},{2,3},{3,2},{4,5},{5,4},{6,7},{7,6},{8,9},{9,8},{10,11... | collective-permute-start | bytes 884744 | tf_op jit(solution)/shard_map/ppermute | solution.py:114
  27.0 0.7 %copy-start.4 = (bf16[128,1152]{1,0:T(8,128)(2,1)}, bf16[128,1152]{1,0:T(8,128)(2,1)S(1)}, u32[]{:S(2)}) copy-start(bf16[128,1152]{1,0:T(8,128)(2,1)S(1)} %collective-permute-done.1.refs_1_) | copy-start | bytes 884740
  45.2 1.6 %copy-start = (bf16[8,16,1152]{2,1,0:T(8,128)(2,1)}, bf16[8,16,1152]{2,1,0:T(8,128)(2,1)S(1)}, u32[]{:S(2)}) copy-start(bf16[8,16,1152]{2,1,0:T(8,128)(2,1)S(1)} %all_to_all.11) | copy-start | bytes 884740
  45.2 1.6 %collective-permute-start.2 = (bf16[128,1152]{1,0:T(8,128)(2,1)S(1)}, bf16[128,1152]{1,0:T(8,128)(2,1)S(1)}, u32[]{:S(2)}, u32[]{:S(2)}) collective-permute-start(bf16[128,1152]{1,0:T(8,128)(2,1)S(1)} %bitcast.7), channel_id=1, source_target_pairs={{0,1},{1,0},{2,3},{3,2},{4,5},{5,4},{6,7},{7,6},{8,9},{9,8},{10,11... | collective-permute-start | bytes 884744 | tf_op jit(solution)/shard_map/ppermute | solution.py:114
  46.7 0.7 %copy-start.3 = (bf16[128,1152]{1,0:T(8,128)(2,1)}, bf16[128,1152]{1,0:T(8,128)(2,1)S(1)}, u32[]{:S(2)}) copy-start(bf16[128,1152]{1,0:T(8,128)(2,1)S(1)} %collective-permute-done.2.refs_1_) | copy-start | bytes 884740

commit v2 on v1

--- a/solution.py
+++ b/solution.py
@@ -106,7 +106,8 @@
 def call(kernel, out, *args):
     spec = pl.BlockSpec(memory_space=pltpu.VMEM)
     return pl.pallas_call(
-        kernel, out_shape=out, in_specs=[spec] * len(args), out_specs=spec
+        kernel, out_shape=out, in_specs=[spec] * len(args), out_specs=spec,
+        compiler_params=pltpu.CompilerParams(vmem_limit_bytes=16 * 2**20),
     )(*args)
 
 

time: 50.9 us -> 42.7 us (0.84)
  Pallas kernels: 12.6 us -> 4.99 us
  blocking collectives: 32 us -> 30.9 us
  waiting for transfers between devices: 3.21 us -> 4.23 us
    pallas_call x5, Pallas kernels: 12.6 us -> 4.99 us  [call(): pl.pallas_call(kernel, out_shape=out, in_specs=[spec] * len(args), out_sp...]
    all_to_all x2, blocking collectives: 32 us -> 30.9 us  [body(): lax.all_to_all(result.reshape(clusters, most, width), ('owner', 'sub'), s...]
    ppermute x3, waiting for transfers between devices: 3.21 us -> 4.23 us  [swap_pair(): return lax.ppermute(values, 'pair', [(0, 1), (1, 0)])]
    unnamed x10 -> x4, local copies, waits for them, and re-layouts: 2.13 us -> 1.74 us
  transfers between devices with their start and end apart: 3 -> 3, of which waited for: 3 -> 3; matrix products, arithmetic and copies ran while one was open for 0% -> 0% of each run, Pallas kernels for 3% -> 0%
where the time goes in v2:
time: 42.7 us; the launch traced here: 42.4 us
  blocking collectives  30.9 us (72%)
  Pallas kernels  4.99 us (12%)
  waiting for transfers between devices  4.23 us (10%)
  local copies, waits for them, and re-layouts  1.74 us (4%)
  starting transfers between devices  0.56 us (1%)
    all_to_all x2, blocking collectives, body(): lax.all_to_all(result.reshape(clusters, most, width), ('owner', 'sub'), s...  30.9 us
    pallas_call x5, Pallas kernels, call(): pl.pallas_call(kernel, out_shape=out, in_specs=[spec] * len(args), out_sp...  4.99 us
    ppermute x3, waiting for transfers between devices, swap_pair(): return lax.ppermute(values, 'pair', [(0, 1), (1, 0)])  4.23 us
    unnamed x4, local copies, waits for them, and re-layouts  1.74 us
  transfers between devices with their start and end apart: 3, of which 3 were waited for; matrix products, arithmetic and copies ran while one was open for 0% of the time, Pallas kernels for 0%

profile of v2, /device:TPU:0, one launch (start us, length us, event | category | flops | bytes accessed | tf_op | source)
XLA Modules:
  0.0 42.4 jit_solution(5381655355136532863)
XLA Ops:
  0.0 0.0 copy-start.1
  0.0 0.7 %copy-done.1 = s32[2,1,1,128]{3,2,1,0:T(1,128)S(1)} copy-done((s32[2,1,1,128]{3,2,1,0:T(1,128)S(1)}, s32[2,1,1,128]{3,2,1,0:T(1,128)}, u32[]{:S(2)}) %copy-start.1) | copy-done | bytes 1048
  0.7 0.0 copy-start
  0.7 1.1 %copy-done = f32[1,1,128,1152]{3,2,1,0:T(8,128)S(1)} copy-done((f32[1,1,128,1152]{3,2,1,0:T(8,128)S(1)}, f32[1,1,128,1152]{3,2,1,0:T(8,128)}, u32[]{:S(2)}) %copy-start) | copy-done | bytes 589848
  1.7 0.2 shard_map.28.refs_0_
  2.0 0.6 %collective-permute-start = (bf16[128,1152]{1,0:T(8,128)(2,1)S(1)}, bf16[128,1152]{1,0:T(8,128)(2,1)S(1)}, u32[]{:S(2)}, u32[]{:S(2)}) collective-permute-start(bf16[128,1152]{1,0:T(8,128)(2,1)S(1)} %shard_map.28.refs_0_), channel_id=1, source_target_pairs={{0,1},{1,0},{2,3},{3,2},{4,5},{5,4},{6,7},{7,6},{8,9},{9,8},{10,11... | collective-permute-start | bytes 884744 | tf_op jit(solution)/shard_map/ppermute | solution.py:115
  2.5 0.1 shard_map.29.refs_2_
  2.6 1.1 %collective-permute-done.refs_1_ = bf16[128,1152]{1,0:T(8,128)(2,1)S(1)} collective-permute-done((bf16[128,1152]{1,0:T(8,128)(2,1)S(1)}, bf16[128,1152]{1,0:T(8,128)(2,1)S(1)}, u32[]{:S(2)}, u32[]{:S(2)}) %collective-permute-start) | collective-permute-done | bytes 294944 | tf_op jit(solution)/shard_map/ppermute | solution.py:115
  3.7 1.2 %shard_map.30 = bf16[128,1152]{1,0:T(8,128)(2,1)S(1)} custom-call(bf16[128,1152]{1,0:T(8,128)(2,1)S(1)} %shard_map.28.refs_0_, bf16[128,1152]{1,0:T(8,128)(2,1)S(1)} %collective-permute-done.refs_1_, s32[2,128]{1,0:T(2,128)S(1)} %shard_map.29.refs_2_), custom_call_target="tpu_custom_call" | custom-call | tf_op jit(solution)/shard_map/pallas_call | solution.py:108
  4.9 17.6 %all_to_all.10 = bf16[8,16,1152]{2,1,0:T(8,128)(2,1)S(1)} all-to-all(bf16[8,16,1152]{2,1,0:T(8,128)(2,1)S(1)} %bitcast.11), channel_id=1, replica_groups=mesh['groups'=2,'owner'=4,'sub'=2,'pair'=2] {'owner','sub'}, dimensions={0} | all-to-all | bytes 589824 | tf_op jit(solution)/shard_map/all_to_all | solution.py:142
  22.5 0.0 collective-permute-start.1
  22.5 1.6 %collective-permute-done.1.refs_1_ = bf16[128,1152]{1,0:T(8,128)(2,1)S(1)} collective-permute-done((bf16[128,1152]{1,0:T(8,128)(2,1)S(1)}, bf16[128,1152]{1,0:T(8,128)(2,1)S(1)}, u32[]{:S(2)}, u32[]{:S(2)}) %collective-permute-start.1) | collective-permute-done | bytes 294944 | tf_op jit(solution)/shard_map/ppermute | solution.py:115
  24.1 1.5 %shard_map.31 = bf16[128,1152]{1,0:T(8,128)(2,1)S(1)} custom-call(bf16[128,1152]{1,0:T(8,128)(2,1)S(1)} %bitcast.10, bf16[128,1152]{1,0:T(8,128)(2,1)S(1)} %collective-permute-done.1.refs_1_, s32[2,128]{1,0:T(2,128)S(1)} %shard_map.29.refs_2_), custom_call_target="tpu_custom_call" | custom-call | tf_op jit(solution)/shard_map/pallas_call | solution.py:108
  25.6 13.3 %all_to_all.11 = bf16[8,16,1152]{2,1,0:T(8,128)(2,1)S(1)} all-to-all(bf16[8,16,1152]{2,1,0:T(8,128)(2,1)S(1)} %bitcast.12), channel_id=1, replica_groups=mesh['groups'=2,'owner'=4,'sub'=2,'pair'=2] {'owner','sub'}, dimensions={0} | all-to-all | bytes 589824 | tf_op jit(solution)/shard_map/all_to_all | solution.py:142
  38.9 0.0 collective-permute-start.2
  38.9 1.6 %collective-permute-done.2.refs_1_ = bf16[128,1152]{1,0:T(8,128)(2,1)S(1)} collective-permute-done((bf16[128,1152]{1,0:T(8,128)(2,1)S(1)}, bf16[128,1152]{1,0:T(8,128)(2,1)S(1)}, u32[]{:S(2)}, u32[]{:S(2)}) %collective-permute-start.2) | collective-permute-done | bytes 294944 | tf_op jit(solution)/shard_map/ppermute | solution.py:115
  40.5 2.0 %shard_map.32 = f32[128,1152]{1,0:T(8,128)} custom-call(bf16[128,1152]{1,0:T(8,128)(2,1)S(1)} %bitcast.8, bf16[128,1152]{1,0:T(8,128)(2,1)S(1)} %collective-permute-done.2.refs_1_, s32[2,128]{1,0:T(2,128)S(1)} %shard_map.29.refs_2_), custom_call_target="tpu_custom_call" | custom-call | tf_op jit(solution)/shard_map/pallas_call | solution.py:108
Async XLA Ops:
  0.0 0.7 %copy-start.1 = (s32[2,1,1,128]{3,2,1,0:T(1,128)S(1)}, s32[2,1,1,128]{3,2,1,0:T(1,128)}, u32[]{:S(2)}) copy-start(s32[2,1,1,128]{3,2,1,0:T(1,128)} %param.3) | copy-start | bytes 3076
  0.7 1.1 %copy-start = (f32[1,1,128,1152]{3,2,1,0:T(8,128)S(1)}, f32[1,1,128,1152]{3,2,1,0:T(8,128)}, u32[]{:S(2)}) copy-start(f32[1,1,128,1152]{3,2,1,0:T(8,128)} %param.2) | copy-start | bytes 1769476
  2.0 1.8 %collective-permute-start = (bf16[128,1152]{1,0:T(8,128)(2,1)S(1)}, bf16[128,1152]{1,0:T(8,128)(2,1)S(1)}, u32[]{:S(2)}, u32[]{:S(2)}) collective-permute-start(bf16[128,1152]{1,0:T(8,128)(2,1)S(1)} %shard_map.28.refs_0_), channel_id=1, source_target_pairs={{0,1},{1,0},{2,3},{3,2},{4,5},{5,4},{6,7},{7,6},{8,9},{9,8},{10,11... | collective-permute-start | bytes 884744 | tf_op jit(solution)/shard_map/ppermute | solution.py:115
  22.5 1.6 %collective-permute-start.1 = (bf16[128,1152]{1,0:T(8,128)(2,1)S(1)}, bf16[128,1152]{1,0:T(8,128)(2,1)S(1)}, u32[]{:S(2)}, u32[]{:S(2)}) collective-permute-start(bf16[128,1152]{1,0:T(8,128)(2,1)S(1)} %bitcast.9), channel_id=1, source_target_pairs={{0,1},{1,0},{2,3},{3,2},{4,5},{5,4},{6,7},{7,6},{8,9},{9,8},{10,11... | collective-permute-start | bytes 884744 | tf_op jit(solution)/shard_map/ppermute | solution.py:115
  38.9 1.6 %collective-permute-start.2 = (bf16[128,1152]{1,0:T(8,128)(2,1)S(1)}, bf16[128,1152]{1,0:T(8,128)(2,1)S(1)}, u32[]{:S(2)}, u32[]{:S(2)}) collective-permute-start(bf16[128,1152]{1,0:T(8,128)(2,1)S(1)} %bitcast.7), channel_id=1, source_target_pairs={{0,1},{1,0},{2,3},{3,2},{4,5},{5,4},{6,7},{7,6},{8,9},{9,8},{10,11... | collective-permute-start | bytes 884744 | tf_op jit(solution)/shard_map/ppermute | solution.py:115

commit v3 on v2

v3 whole, which is shorter than its diff:
```python
import jax
import jax.numpy as jnp
from jax import lax
from jax.experimental import pallas as pl
from jax.experimental.pallas import tpu as pltpu
from jax.sharding import PartitionSpec as P


PASSES = 3
SHARES = 2
LANES = 128
MARK = 2.0


epsilon = 1e-06
sharpness = 6.0

f32 = jnp.float32
bf16 = jnp.bfloat16
i32 = jnp.int32


def offset_of(clusters, step, core):
    return clusters - 1 - 2 * step - (core ^ (step & 1))


def here():
    cluster = lax.axis_index("owner") * lax.axis_size("sub") + lax.axis_index("sub")
    return cluster, lax.axis_index("pair")


def iota(shape, axis):
    return lax.broadcasted_iota(i32, shape, axis)


def mark_empty(head, live):
    return jnp.where((iota(head.shape, 1) == 0) & jnp.logical_not(live), MARK, head)


def state_kernel(emb_ref, moves_ref, out_ref):
    rows = emb_ref.shape[0]
    values = emb_ref[...]
    count = jnp.sum((moves_ref[0:1, :] >= 0).astype(f32), axis=1, keepdims=True)
    live = iota((rows, 1), 0).astype(f32) < count
    total = jnp.sum(values * values, axis=1, keepdims=True)
    unit = jnp.where(live, values * lax.rsqrt(total + epsilon), 0.0)
    out_ref[:, LANES:] = unit[:, LANES:].astype(bf16)
    out_ref[:, :LANES] = mark_empty(unit[:, :LANES], live).astype(bf16)


def places_kernel(clusters, most, own_ref, peer_ref, out_ref):
    lists, rows = own_ref.shape
    cluster, core = here()
    before = (iota((rows, rows), 0) < iota((rows, rows), 1)).astype(bf16)
    for number in range(lists):
        for half, ref in enumerate((own_ref, peer_ref)):
            targets = ref[number : number + 1, :]
            onehot = (iota((clusters, rows), 0) == targets).astype(f32)
            earlier = jnp.dot(onehot.astype(bf16), before, preferred_element_type=f32)
            rank = jnp.sum(onehot * earlier, axis=0, keepdims=True).astype(i32)
            back = clusters - 1 - (targets ^ cluster)
            step = back >> 1
            mine = ((back & 1) ^ (step & 1)) == core
            place = (step * SHARES + (core ^ half)) * most + rank
            out_ref[number : number + 1, half * rows : (half + 1) * rows] = jnp.where(
                (targets >= 0) & mine, place, -1
            )


def pass_kernel(clusters, most, number, last, count, *refs):
    blocks, (places_ref, *outs) = refs[:count], refs[count:]
    width = blocks[0].shape[1]
    total_rows = count * blocks[0].shape[0]
    rows = total_rows // SHARES
    block = SHARES * most
    cluster, core = here()

    heads = jnp.concatenate([ref[:, :LANES] for ref in blocks], axis=0).astype(f32)
    live = jnp.broadcast_to((heads[:, 0:1] < 1.5).astype(f32), (total_rows, LANES))
    heads = jnp.where(live > 0.5, heads, 0.0).astype(bf16)
    tails = jnp.concatenate([ref[:, LANES:] for ref in blocks], axis=0)
    keys = jnp.concatenate([heads, tails], axis=1)
    flags = live.astype(bf16)

    if number == 0:
        place = places_ref[number : number + 1, :]
        select = (iota((rows, total_rows), 0) == place).astype(bf16)
    else:

        def order(index):
            half = (index >= rows).astype(i32)
            inner = index - half * rows
            step = inner // block
            share = (inner // most) & 1
            source = cluster ^ offset_of(clusters, step, core ^ half)
            return share, share * (4 * rows) + source * most + inner % most

        share, key = order(iota((total_rows, 1), 0))
        _, other = order(iota((1, total_rows), 1))
        ahead = key - other
        ahead = ((ahead > 0) & (ahead < 2 * rows)).astype(bf16)
        slot = jnp.dot(ahead, flags, preferred_element_type=f32)
        slot = jnp.where(live > 0.5, slot, -1.0)[:, 0:1]
        lane = iota((total_rows, rows), 1).astype(f32)
        own = (share == core).astype(f32)
        mine = ((slot == lane) & (own > 0.5)).astype(bf16)
        if last:
            wanted = (iota((rows, rows), 0) == iota((rows, rows), 1)).astype(bf16)
        else:
            theirs = ((slot == lane) & (own < 0.5)).astype(bf16)
            mine = jnp.concatenate([mine, theirs], axis=1)
            place = places_ref[number : number + 1, :]
            wanted = (iota((rows, total_rows), 0) == place).astype(bf16)
        select = lax.dot_general(
            wanted, mine, (((1,), (1,)), ((), ())), preferred_element_type=f32
        ).astype(bf16)

    scores = lax.dot_general(keys, keys, (((1,), (1,)), ((), ())), preferred_element_type=f32)
    weights = jnp.exp(sharpness * (scores - 1.0)).astype(bf16)
    chosen = jnp.dot(select, weights, preferred_element_type=f32).astype(bf16)
    sums = jnp.dot(
        chosen, jnp.concatenate([keys, flags], axis=1), preferred_element_type=f32
    )
    numer = sums[:, :width]
    denom = sums[:, width : width + 1]
    found = denom > 0.0
    inverse = 1.0 / jnp.where(found, denom, 1.0)
    total = jnp.sum(numer * numer, axis=1, keepdims=True)
    scale = inverse * lax.rsqrt(total * (inverse * inverse) + epsilon)
    unit = jnp.where(found, numer * scale, 0.0)
    if last:
        outs[0][...] = unit
        return
    head = mark_empty(unit[:, :LANES], found).astype(bf16)
    tail = unit[:, LANES:].astype(bf16)
    size = outs[0].shape[0]
    for index, out in enumerate(outs):
        out[:, :LANES] = head[index * size : (index + 1) * size]
        out[:, LANES:] = tail[index * size : (index + 1) * size]


def call(kernel, out, *args):
    spec = pl.BlockSpec(memory_space=pltpu.VMEM)
    return pl.pallas_call(
        kernel,
        out_shape=out,
        in_specs=[spec] * len(args),
        out_specs=jax.tree.map(lambda _: spec, out),
        compiler_params=pltpu.CompilerParams(vmem_limit_bytes=16 * 2**20),
    )(*args)


def swap_pair(values):
    return lax.ppermute(values, "pair", [(0, 1), (1, 0)])


def send(values, clusters, step):
    pairs = [
        (cluster * 2 + core, (cluster ^ offset_of(clusters, step, core)) * 2 + core)
        for cluster in range(clusters)
        for core in range(2)
    ]
    return lax.ppermute(values, ("owner", "sub", "pair"), pairs)


def body(embeddings, moves):
    rows, width = embeddings.shape[2:]
    clusters = lax.axis_size("owner") * lax.axis_size("sub")
    most = rows // clusters
    steps = clusters // 2
    block = SHARES * most
    aligned = block % 16 == 0
    targets = moves[:, 0, 0, :]
    peer_targets = swap_pair(targets)
    state = call(
        state_kernel, jax.ShapeDtypeStruct((rows, width), bf16), embeddings[0, 0], targets
    )
    places = call(
        lambda *refs: places_kernel(clusters, most, *refs),
        jax.ShapeDtypeStruct((targets.shape[0], SHARES * rows), i32),
        targets,
        peer_targets,
    )
    keys = [state, swap_pair(state)]
    for number in range(PASSES):
        last = number + 1 == PASSES
        if last:
            out = jax.ShapeDtypeStruct((rows, width), f32)
        elif aligned:
            out = [jax.ShapeDtypeStruct((block, width), bf16)] * steps
        else:
            out = [jax.ShapeDtypeStruct((rows, width), bf16)]
        result = call(
            lambda *refs: pass_kernel(clusters, most, number, last, len(keys), *refs),
            out,
            *keys,
            places,
        )
        if last:
            return result[None, None]
        if not aligned:
            result = [result[0][step * block : (step + 1) * block] for step in range(steps)]
        far, near = [], []
        for step in range(steps):
            far.append(send(result[step], clusters, step))
        for step in range(steps):
            near.append(swap_pair(far[step]))
        if aligned:
            keys = far + near
        else:
            keys = [jnp.concatenate(far, axis=0), jnp.concatenate(near, axis=0)]


def solution(mesh):
    placed = (
        P(("groups", "owner", "sub"), "pair", None, None),
        P(None, ("groups", "owner", "sub"), "pair", None),
    )
    return jax.shard_map(
        body,
        mesh=mesh,
        in_specs=placed,
        out_specs=P(("groups", "owner", "sub"), "pair", None, None),
        check_vma=False,
    )
```

time: 42.7 us -> 34.1 us (0.80)
  blocking collectives: 30.9 us -> 0 us
  starting transfers between devices: 0.56 us -> 15.2 us
  waiting for transfers between devices: 4.23 us -> 12 us
    all_to_all x2 -> x0, blocking collectives: 30.9 us -> none  [body(): lax.all_to_all(result.reshape(clusters, most, width), ('owner', 'sub'), s...]
    ppermute x0 -> x8, starting transfers between devices: none -> 13.2 us  [send(): return lax.ppermute(values, ('owner', 'sub', 'pair'), pairs)]
    ppermute x0 -> x8, waiting for transfers between devices: none -> 8.98 us  [send(): return lax.ppermute(values, ('owner', 'sub', 'pair'), pairs)]
    ppermute x3 -> x10, starting transfers between devices: 0.56 us -> 1.95 us  [swap_pair(): return lax.ppermute(values, 'pair', [(0, 1), (1, 0)])]
    ppermute x3 -> x10, waiting for transfers between devices: 4.23 us -> 3.04 us  [swap_pair(): return lax.ppermute(values, 'pair', [(0, 1), (1, 0)])]
  transfers between devices with their start and end apart: 3 -> 18, of which waited for: 3 -> 11; matrix products, arithmetic and copies ran while one was open for 0% -> 0% of each run, Pallas kernels for 0% -> 0%
where the time goes in v3:
time: 34.1 us; the launch traced here: 33.9 us
  starting transfers between devices  15.2 us (45%)
  waiting for transfers between devices  12 us (35%)
  Pallas kernels  4.85 us (14%)
  local copies, waits for them, and re-layouts  1.74 us (5%)
    ppermute x8, starting transfers between devices, send(): return lax.ppermute(values, ('owner', 'sub', 'pair'), pairs)  13.2 us
    ppermute x8, waiting for transfers between devices, send(): return lax.ppermute(values, ('owner', 'sub', 'pair'), pairs)  8.98 us
    pallas_call x5, Pallas kernels, call(): pl.pallas_call(kernel, out_shape=out, in_specs=[spec] * len(args), out_sp...  4.85 us
    ppermute x10, waiting for transfers between devices, swap_pair(): return lax.ppermute(values, 'pair', [(0, 1), (1, 0)])  3.04 us
    ppermute x10, starting transfers between devices, swap_pair(): return lax.ppermute(values, 'pair', [(0, 1), (1, 0)])  1.95 us
    unnamed x4, local copies, waits for them, and re-layouts  1.74 us
  transfers between devices with their start and end apart: 18, of which 11 were waited for; matrix products, arithmetic and copies ran while one was open for 0% of the time, Pallas kernels for 0%

profile of v3, /device:TPU:0, one launch (start us, length us, event | category | flops | bytes accessed | tf_op | source)
XLA Modules:
  0.0 33.9 jit_solution(7629943724165250697)
XLA Ops:
  0.0 0.0 copy-start.1
  0.0 0.7 %copy-done.1 = s32[2,1,1,128]{3,2,1,0:T(1,128)S(1)} copy-done((s32[2,1,1,128]{3,2,1,0:T(1,128)S(1)}, s32[2,1,1,128]{3,2,1,0:T(1,128)}, u32[]{:S(2)}) %copy-start.1) | copy-done | bytes 1048
  0.7 0.0 copy-start
  0.7 1.1 %copy-done = f32[1,1,128,1152]{3,2,1,0:T(8,128)S(1)} copy-done((f32[1,1,128,1152]{3,2,1,0:T(8,128)S(1)}, f32[1,1,128,1152]{3,2,1,0:T(8,128)}, u32[]{:S(2)}) %copy-start) | copy-done | bytes 589848
  1.7 0.2 shard_map.28.refs_0_
  1.9 0.6 %collective-permute-start = (bf16[128,1152]{1,0:T(8,128)(2,1)S(1)}, bf16[128,1152]{1,0:T(8,128)(2,1)S(1)}, u32[]{:S(2)}, u32[]{:S(2)}) collective-permute-start(bf16[128,1152]{1,0:T(8,128)(2,1)S(1)} %shard_map.28.refs_0_), channel_id=1, source_target_pairs={{0,1},{1,0},{2,3},{3,2},{4,5},{5,4},{6,7},{7,6},{8,9},{9,8},{10,11... | collective-permute-start | bytes 884744 | tf_op jit(solution)/shard_map/ppermute | solution.py:154
  2.5 0.1 collective-permute-start.1
  2.6 1.1 %collective-permute-done.1.refs_1_ = s32[2,128]{1,0:T(2,128)S(1)} collective-permute-done((s32[2,128]{1,0:T(2,128)S(1)}, s32[2,128]{1,0:T(2,128)S(1)}, u32[]{:S(2)}, u32[]{:S(2)}) %collective-permute-start.1) | collective-permute-done | bytes 1056 | tf_op jit(solution)/shard_map/ppermute | solution.py:154
  3.7 0.2 shard_map.29.refs_2_.refs_8_
  3.9 0.0 collective-permute-done.refs_1_
  3.9 1.2 %shard_map.30 = (bf16[32,1152]{1,0:T(8,128)(2,1)S(1)}, bf16[32,1152]{1,0:T(8,128)(2,1)S(1)}, bf16[32,1152]{1,0:T(8,128)(2,1)S(1)}, bf16[32,1152]{1,0:T(8,128)(2,1)S(1)}) custom-call(bf16[128,1152]{1,0:T(8,128)(2,1)S(1)} %shard_map.28.refs_0_, bf16[128,1152]{1,0:T(8,128)(2,1)S(1)} %collective-permute-done.refs_1_, s32[2,256]{1,0:T(2,128)S(1)} %shard_map.29.refs_2_.refs_8_), custom_call_target="tpu_custom_call" | custom-call | tf_op jit(solution)/shard_map/pallas_call | solution.py:144
  5.1 6.0 %collective-permute-start.2 = (bf16[32,1152]{1,0:T(8,128)(2,1)S(1)}, bf16[32,1152]{1,0:T(8,128)(2,1)S(1)}, u32[]{:S(2)}, u32[]{:S(2)}) collective-permute-start(bf16[32,1152]{1,0:T(8,128)(2,1)S(1)} %get-tuple-element.13), channel_id=1, source_target_pairs={{0,14},{1,13},{2,12},{3,15},{4,10},{5,9},{6,8},{7,11},{8,6},{9,5},... | collective-permute-start | bytes 221192 | tf_op jit(solution)/shard_map/ppermute | solution.py:163
  11.0 0.0 collective-permute-start.3
  11.0 0.6 %collective-permute-start.4 = (bf16[32,1152]{1,0:T(8,128)(2,1)S(1)}, bf16[32,1152]{1,0:T(8,128)(2,1)S(1)}, u32[]{:S(2)}, u32[]{:S(2)}) collective-permute-start(bf16[32,1152]{1,0:T(8,128)(2,1)S(1)} %get-tuple-element.15), channel_id=1, source_target_pairs={{0,6},{1,5},{2,4},{3,7},{4,2},{5,1},{6,0},{7,3},{8,14},{9,13},{10,... | collective-permute-start | bytes 221192 | tf_op jit(solution)/shard_map/ppermute | solution.py:163
  11.7 0.7 %collective-permute-start.5 = (bf16[32,1152]{1,0:T(8,128)(2,1)S(1)}, bf16[32,1152]{1,0:T(8,128)(2,1)S(1)}, u32[]{:S(2)}, u32[]{:S(2)}) collective-permute-start(bf16[32,1152]{1,0:T(8,128)(2,1)S(1)} %get-tuple-element.16), channel_id=1, source_target_pairs={{0,0},{1,3},{2,2},{3,1},{4,4},{5,7},{6,6},{7,5},{8,8},{9,11},{10,1... | collective-permute-start | bytes 221192 | tf_op jit(solution)/shard_map/ppermute | solution.py:163
  12.3 1.7 %collective-permute-done.2.refs_0_ = bf16[32,1152]{1,0:T(8,128)(2,1)S(1)} collective-permute-done((bf16[32,1152]{1,0:T(8,128)(2,1)S(1)}, bf16[32,1152]{1,0:T(8,128)(2,1)S(1)}, u32[]{:S(2)}, u32[]{:S(2)}) %collective-permute-start.2) | collective-permute-done | bytes 73760 | tf_op jit(solution)/shard_map/ppermute | solution.py:163
  14.0 0.0 collective-permute-start.6
  14.0 2.8 %collective-permute-done.3.refs_1_ = bf16[32,1152]{1,0:T(8,128)(2,1)S(1)} collective-permute-done((bf16[32,1152]{1,0:T(8,128)(2,1)S(1)}, bf16[32,1152]{1,0:T(8,128)(2,1)S(1)}, u32[]{:S(2)}, u32[]{:S(2)}) %collective-permute-start.3) | collective-permute-done | bytes 73760 | tf_op jit(solution)/shard_map/ppermute | solution.py:163
  16.7 0.0 collective-permute-start.7
  16.8 1.0 %collective-permute-done.4.refs_2_ = bf16[32,1152]{1,0:T(8,128)(2,1)S(1)} collective-permute-done((bf16[32,1152]{1,0:T(8,128)(2,1)S(1)}, bf16[32,1152]{1,0:T(8,128)(2,1)S(1)}, u32[]{:S(2)}, u32[]{:S(2)}) %collective-permute-start.4) | collective-permute-done | bytes 73760 | tf_op jit(solution)/shard_map/ppermute | solution.py:163
  17.7 0.0 collective-permute-start.8
  17.7 0.0 collective-permute-done.5.refs_3_
  17.8 0.5 %collective-permute-start.9 = (bf16[32,1152]{1,0:T(8,128)(2,1)S(1)}, bf16[32,1152]{1,0:T(8,128)(2,1)S(1)}, u32[]{:S(2)}, u32[]{:S(2)}) collective-permute-start(bf16[32,1152]{1,0:T(8,128)(2,1)S(1)} %collective-permute-done.5.refs_3_), channel_id=1, source_target_pairs={{0,1},{1,0},{2,3},{3,2},{4,5},{5,4},{6,7},{7,6},{8,9},{9,8},{10,11... | collective-permute-start | bytes 221192 | tf_op jit(solution)/shard_map/ppermute | solution.py:154
  18.3 0.0 collective-permute-done.6.refs_4_
  18.3 0.0 collective-permute-done.7.refs_5_
  18.3 0.7 %collective-permute-done.8.refs_6_ = bf16[32,1152]{1,0:T(8,128)(2,1)S(1)} collective-permute-done((bf16[32,1152]{1,0:T(8,128)(2,1)S(1)}, bf16[32,1152]{1,0:T(8,128)(2,1)S(1)}, u32[]{:S(2)}, u32[]{:S(2)}) %collective-permute-start.8) | collective-permute-done | bytes 73760 | tf_op jit(solution)/shard_map/ppermute | solution.py:154
  19.0 0.2 collective-permute-done.9.refs_7_
  19.2 1.3 %shard_map.31 = (bf16[32,1152]{1,0:T(8,128)(2,1)S(1)}, bf16[32,1152]{1,0:T(8,128)(2,1)S(1)}, bf16[32,1152]{1,0:T(8,128)(2,1)S(1)}, bf16[32,1152]{1,0:T(8,128)(2,1)S(1)}) custom-call(bf16[32,1152]{1,0:T(8,128)(2,1)S(1)} %collective-permute-done.2.refs_0_, bf16[32,1152]{1,0:T(8,128)(2,1)S(1)} %collective-permute-done.3.refs_1_, ...), custom_call_target="tpu_custom_call" | custom-call | tf_op jit(solution)/shard_map/pallas_call | solution.py:144
  20.5 2.6 %collective-permute-start.10 = (bf16[32,1152]{1,0:T(8,128)(2,1)S(1)}, bf16[32,1152]{1,0:T(8,128)(2,1)S(1)}, u32[]{:S(2)}, u32[]{:S(2)}) collective-permute-start(bf16[32,1152]{1,0:T(8,128)(2,1)S(1)} %get-tuple-element.17), channel_id=1, source_target_pairs={{0,14},{1,13},{2,12},{3,15},{4,10},{5,9},{6,8},{7,11},{8,6},{9,5},... | collective-permute-start | bytes 221192 | tf_op jit(solution)/shard_map/ppermute | solution.py:163
  23.2 0.0 collective-permute-start.11
  23.2 2.7 %collective-permute-start.12 = (bf16[32,1152]{1,0:T(8,128)(2,1)S(1)}, bf16[32,1152]{1,0:T(8,128)(2,1)S(1)}, u32[]{:S(2)}, u32[]{:S(2)}) collective-permute-start(bf16[32,1152]{1,0:T(8,128)(2,1)S(1)} %get-tuple-element.19), channel_id=1, source_target_pairs={{0,6},{1,5},{2,4},{3,7},{4,2},{5,1},{6,0},{7,3},{8,14},{9,13},{10,... | collective-permute-start | bytes 221192 | tf_op jit(solution)/shard_map/ppermute | solution.py:163
  25.9 0.7 %collective-permute-start.13 = (bf16[32,1152]{1,0:T(8,128)(2,1)S(1)}, bf16[32,1152]{1,0:T(8,128)(2,1)S(1)}, u32[]{:S(2)}, u32[]{:S(2)}) collective-permute-start(bf16[32,1152]{1,0:T(8,128)(2,1)S(1)} %get-tuple-element.20), channel_id=1, source_target_pairs={{0,0},{1,3},{2,2},{3,1},{4,4},{5,7},{6,6},{7,5},{8,8},{9,11},{10,1... | collective-permute-start | bytes 221192 | tf_op jit(solution)/shard_map/ppermute | solution.py:163
  26.5 1.8 %collective-permute-done.10.refs_0_ = bf16[32,1152]{1,0:T(8,128)(2,1)S(1)} collective-permute-done((bf16[32,1152]{1,0:T(8,128)(2,1)S(1)}, bf16[32,1152]{1,0:T(8,128)(2,1)S(1)}, u32[]{:S(2)}, u32[]{:S(2)}) %collective-permute-start.10) | collective-permute-done | bytes 73760 | tf_op jit(solution)/shard_map/ppermute | solution.py:163
  28.3 0.0 collective-permute-start.14
  28.3 1.8 %collective-permute-done.11.refs_1_ = bf16[32,1152]{1,0:T(8,128)(2,1)S(1)} collective-permute-done((bf16[32,1152]{1,0:T(8,128)(2,1)S(1)}, bf16[32,1152]{1,0:T(8,128)(2,1)S(1)}, u32[]{:S(2)}, u32[]{:S(2)}) %collective-permute-start.11) | collective-permute-done | bytes 73760 | tf_op jit(solution)/shard_map/ppermute | solution.py:163
  30.1 0.3 collective-permute-start.15
  30.4 0.0 collective-permute-done.12.refs_2_
  30.4 0.2 collective-permute-start.16
  30.6 0.0 collective-permute-done.13.refs_3_
  30.6 0.3 collective-permute-start.17
  30.9 0.0 collective-permute-done.14.refs_4_
  30.9 0.5 %collective-permute-done.15.refs_5_ = bf16[32,1152]{1,0:T(8,128)(2,1)S(1)} collective-permute-done((bf16[32,1152]{1,0:T(8,128)(2,1)S(1)}, bf16[32,1152]{1,0:T(8,128)(2,1)S(1)}, u32[]{:S(2)}, u32[]{:S(2)}) %collective-permute-start.15) | collective-permute-done | bytes 73760 | tf_op jit(solution)/shard_map/ppermute | solution.py:154
  31.4 0.3 collective-permute-done.16.refs_6_
  31.6 0.2 collective-permute-done.17.refs_7_
  31.9 2.0 %shard_map.32 = f32[128,1152]{1,0:T(8,128)} custom-call(bf16[32,1152]{1,0:T(8,128)(2,1)S(1)} %collective-permute-done.10.refs_0_, bf16[32,1152]{1,0:T(8,128)(2,1)S(1)} %collective-permute-done.11.refs_1_, bf16[32,1152]{1,0:T(8,128)(2,1)S(1)} %collective-permute-done.12.refs_2_, bf16[32,1152]{1,0:T(8,128)(2,1)S(1)} %collective-permute-done.13.refs_3_, ...), custom_call_target="tpu_custom_call" | custom-call | tf_op jit(solution)/shard_map/pallas_call | solution.py:144
Async XLA Ops:
  0.0 0.7 %copy-start.1 = (s32[2,1,1,128]{3,2,1,0:T(1,128)S(1)}, s32[2,1,1,128]{3,2,1,0:T(1,128)}, u32[]{:S(2)}) copy-start(s32[2,1,1,128]{3,2,1,0:T(1,128)} %param.3) | copy-start | bytes 3076
  0.7 1.1 %copy-start = (f32[1,1,128,1152]{3,2,1,0:T(8,128)S(1)}, f32[1,1,128,1152]{3,2,1,0:T(8,128)}, u32[]{:S(2)}) copy-start(f32[1,1,128,1152]{3,2,1,0:T(8,128)} %param.2) | copy-start | bytes 1769476
  1.9 1.9 %collective-permute-start = (bf16[128,1152]{1,0:T(8,128)(2,1)S(1)}, bf16[128,1152]{1,0:T(8,128)(2,1)S(1)}, u32[]{:S(2)}, u32[]{:S(2)}) collective-permute-start(bf16[128,1152]{1,0:T(8,128)(2,1)S(1)} %shard_map.28.refs_0_), channel_id=1, source_target_pairs={{0,1},{1,0},{2,3},{3,2},{4,5},{5,4},{6,7},{7,6},{8,9},{9,8},{10,11... | collective-permute-start | bytes 884744 | tf_op jit(solution)/shard_map/ppermute | solution.py:154
  2.5 1.2 %collective-permute-start.1 = (s32[2,128]{1,0:T(2,128)S(1)}, s32[2,128]{1,0:T(2,128)S(1)}, u32[]{:S(2)}, u32[]{:S(2)}) collective-permute-start(s32[2,128]{1,0:T(2,128)S(1)} %bitcast.5), channel_id=1, source_target_pairs={{0,1},{1,0},{2,3},{3,2},{4,5},{5,4},{6,7},{7,6},{8,9},{9,8},{10,11... | collective-permute-start | bytes 3080 | tf_op jit(solution)/shard_map/ppermute | solution.py:154
  5.1 8.9 %collective-permute-start.2 = (bf16[32,1152]{1,0:T(8,128)(2,1)S(1)}, bf16[32,1152]{1,0:T(8,128)(2,1)S(1)}, u32[]{:S(2)}, u32[]{:S(2)}) collective-permute-start(bf16[32,1152]{1,0:T(8,128)(2,1)S(1)} %get-tuple-element.13), channel_id=1, source_target_pairs={{0,14},{1,13},{2,12},{3,15},{4,10},{5,9},{6,8},{7,11},{8,6},{9,5},... | collective-permute-start | bytes 221192 | tf_op jit(solution)/shard_map/ppermute | solution.py:163
  11.0 5.7 %collective-permute-start.3 = (bf16[32,1152]{1,0:T(8,128)(2,1)S(1)}, bf16[32,1152]{1,0:T(8,128)(2,1)S(1)}, u32[]{:S(2)}, u32[]{:S(2)}) collective-permute-start(bf16[32,1152]{1,0:T(8,128)(2,1)S(1)} %get-tuple-element.14), channel_id=1, source_target_pairs={{0,8},{1,11},{2,10},{3,9},{4,12},{5,15},{6,14},{7,13},{8,0},{9,3},... | collective-permute-start | bytes 221192 | tf_op jit(solution)/shard_map/ppermute | solution.py:163
  11.0 6.7 %collective-permute-start.4 = (bf16[32,1152]{1,0:T(8,128)(2,1)S(1)}, bf16[32,1152]{1,0:T(8,128)(2,1)S(1)}, u32[]{:S(2)}, u32[]{:S(2)}) collective-permute-start(bf16[32,1152]{1,0:T(8,128)(2,1)S(1)} %get-tuple-element.15), channel_id=1, source_target_pairs={{0,6},{1,5},{2,4},{3,7},{4,2},{5,1},{6,0},{7,3},{8,14},{9,13},{10,... | collective-permute-start | bytes 221192 | tf_op jit(solution)/shard_map/ppermute | solution.py:163
  11.7 6.1 %collective-permute-start.5 = (bf16[32,1152]{1,0:T(8,128)(2,1)S(1)}, bf16[32,1152]{1,0:T(8,128)(2,1)S(1)}, u32[]{:S(2)}, u32[]{:S(2)}) collective-permute-start(bf16[32,1152]{1,0:T(8,128)(2,1)S(1)} %get-tuple-element.16), channel_id=1, source_target_pairs={{0,0},{1,3},{2,2},{3,1},{4,4},{5,7},{6,6},{7,5},{8,8},{9,11},{10,1... | collective-permute-start | bytes 221192 | tf_op jit(solution)/shard_map/ppermute | solution.py:163
  14.0 4.3 %collective-permute-start.6 = (bf16[32,1152]{1,0:T(8,128)(2,1)S(1)}, bf16[32,1152]{1,0:T(8,128)(2,1)S(1)}, u32[]{:S(2)}, u32[]{:S(2)}) collective-permute-start(bf16[32,1152]{1,0:T(8,128)(2,1)S(1)} %collective-permute-done.2.refs_0_), channel_id=1, source_target_pairs={{0,1},{1,0},{2,3},{3,2},{4,5},{5,4},{6,7},{7,6},{8,9},{9,8},{10,11... | collective-permute-start | bytes 221192 | tf_op jit(solution)/shard_map/ppermute | solution.py:154
  16.7 1.5 %collective-permute-start.7 = (bf16[32,1152]{1,0:T(8,128)(2,1)S(1)}, bf16[32,1152]{1,0:T(8,128)(2,1)S(1)}, u32[]{:S(2)}, u32[]{:S(2)}) collective-permute-start(bf16[32,1152]{1,0:T(8,128)(2,1)S(1)} %collective-permute-done.3.refs_1_), channel_id=1, source_target_pairs={{0,1},{1,0},{2,3},{3,2},{4,5},{5,4},{6,7},{7,6},{8,9},{9,8},{10,11... | collective-permute-start | bytes 221192 | tf_op jit(solution)/shard_map/ppermute | solution.py:154
  17.7 1.3 %collective-permute-start.8 = (bf16[32,1152]{1,0:T(8,128)(2,1)S(1)}, bf16[32,1152]{1,0:T(8,128)(2,1)S(1)}, u32[]{:S(2)}, u32[]{:S(2)}) collective-permute-start(bf16[32,1152]{1,0:T(8,128)(2,1)S(1)} %collective-permute-done.4.refs_2_), channel_id=1, source_target_pairs={{0,1},{1,0},{2,3},{3,2},{4,5},{5,4},{6,7},{7,6},{8,9},{9,8},{10,11... | collective-permute-start | bytes 221192 | tf_op jit(solution)/shard_map/ppermute | solution.py:154
  17.8 1.4 %collective-permute-start.9 = (bf16[32,1152]{1,0:T(8,128)(2,1)S(1)}, bf16[32,1152]{1,0:T(8,128)(2,1)S(1)}, u32[]{:S(2)}, u32[]{:S(2)}) collective-permute-start(bf16[32,1152]{1,0:T(8,128)(2,1)S(1)} %collective-permute-done.5.refs_3_), channel_id=1, source_target_pairs={{0,1},{1,0},{2,3},{3,2},{4,5},{5,4},{6,7},{7,6},{8,9},{9,8},{10,11... | collective-permute-start | bytes 221192 | tf_op jit(solution)/shard_map/ppermute | solution.py:154
  20.5 7.8 %collective-permute-start.10 = (bf16[32,1152]{1,0:T(8,128)(2,1)S(1)}, bf16[32,1152]{1,0:T(8,128)(2,1)S(1)}, u32[]{:S(2)}, u32[]{:S(2)}) collective-permute-start(bf16[32,1152]{1,0:T(8,128)(2,1)S(1)} %get-tuple-element.17), channel_id=1, source_target_pairs={{0,14},{1,13},{2,12},{3,15},{4,10},{5,9},{6,8},{7,11},{8,6},{9,5},... | collective-permute-start | bytes 221192 | tf_op jit(solution)/shard_map/ppermute | solution.py:163
  23.2 6.9 %collective-permute-start.11 = (bf16[32,1152]{1,0:T(8,128)(2,1)S(1)}, bf16[32,1152]{1,0:T(8,128)(2,1)S(1)}, u32[]{:S(2)}, u32[]{:S(2)}) collective-permute-start(bf16[32,1152]{1,0:T(8,128)(2,1)S(1)} %get-tuple-element.18), channel_id=1, source_target_pairs={{0,8},{1,11},{2,10},{3,9},{4,12},{5,15},{6,14},{7,13},{8,0},{9,3},... | collective-permute-start | bytes 221192 | tf_op jit(solution)/shard_map/ppermute | solution.py:163
  23.2 7.2 %collective-permute-start.12 = (bf16[32,1152]{1,0:T(8,128)(2,1)S(1)}, bf16[32,1152]{1,0:T(8,128)(2,1)S(1)}, u32[]{:S(2)}, u32[]{:S(2)}) collective-permute-start(bf16[32,1152]{1,0:T(8,128)(2,1)S(1)} %get-tuple-element.19), channel_id=1, source_target_pairs={{0,6},{1,5},{2,4},{3,7},{4,2},{5,1},{6,0},{7,3},{8,14},{9,13},{10,... | collective-permute-start | bytes 221192 | tf_op jit(solution)/shard_map/ppermute | solution.py:163
  25.9 4.8 %collective-permute-start.13 = (bf16[32,1152]{1,0:T(8,128)(2,1)S(1)}, bf16[32,1152]{1,0:T(8,128)(2,1)S(1)}, u32[]{:S(2)}, u32[]{:S(2)}) collective-permute-start(bf16[32,1152]{1,0:T(8,128)(2,1)S(1)} %get-tuple-element.20), channel_id=1, source_target_pairs={{0,0},{1,3},{2,2},{3,1},{4,4},{5,7},{6,6},{7,5},{8,8},{9,11},{10,1... | collective-permute-start | bytes 221192 | tf_op jit(solution)/shard_map/ppermute | solution.py:163
  28.3 2.6 %collective-permute-start.14 = (bf16[32,1152]{1,0:T(8,128)(2,1)S(1)}, bf16[32,1152]{1,0:T(8,128)(2,1)S(1)}, u32[]{:S(2)}, u32[]{:S(2)}) collective-permute-start(bf16[32,1152]{1,0:T(8,128)(2,1)S(1)} %collective-permute-done.10.refs_0_), channel_id=1, source_target_pairs={{0,1},{1,0},{2,3},{3,2},{4,5},{5,4},{6,7},{7,6},{8,9},{9,8},{10,11... | collective-permute-start | bytes 221192 | tf_op jit(solution)/shard_map/ppermute | solution.py:154
  30.1 1.3 %collective-permute-start.15 = (bf16[32,1152]{1,0:T(8,128)(2,1)S(1)}, bf16[32,1152]{1,0:T(8,128)(2,1)S(1)}, u32[]{:S(2)}, u32[]{:S(2)}) collective-permute-start(bf16[32,1152]{1,0:T(8,128)(2,1)S(1)} %collective-permute-done.11.refs_1_), channel_id=1, source_target_pairs={{0,1},{1,0},{2,3},{3,2},{4,5},{5,4},{6,7},{7,6},{8,9},{9,8},{10,11... | collective-permute-start | bytes 221192 | tf_op jit(solution)/shard_map/ppermute | solution.py:154
  30.4 1.3 %collective-permute-start.16 = (bf16[32,1152]{1,0:T(8,128)(2,1)S(1)}, bf16[32,1152]{1,0:T(8,128)(2,1)S(1)}, u32[]{:S(2)}, u32[]{:S(2)}) collective-permute-start(bf16[32,1152]{1,0:T(8,128)(2,1)S(1)} %collective-permute-done.12.refs_2_), channel_id=1, source_target_pairs={{0,1},{1,0},{2,3},{3,2},{4,5},{5,4},{6,7},{7,6},{8,9},{9,8},{10,11... | collective-permute-start | bytes 221192 | tf_op jit(solution)/shard_map/ppermute | solution.py:154
  30.6 1.3 %collective-permute-start.17 = (bf16[32,1152]{1,0:T(8,128)(2,1)S(1)}, bf16[32,1152]{1,0:T(8,128)(2,1)S(1)}, u32[]{:S(2)}, u32[]{:S(2)}) collective-permute-start(bf16[32,1152]{1,0:T(8,128)(2,1)S(1)} %collective-permute-done.13.refs_3_), channel_id=1, source_target_pairs={{0,1},{1,0},{2,3},{3,2},{4,5},{5,4},{6,7},{7,6},{8,9},{9,8},{10,11... | collective-permute-start | bytes 221192 | tf_op jit(solution)/shard_map/ppermute | solution.py:154

commit v4 on v3

--- a/solution.py
+++ b/solution.py
@@ -37,18 +37,20 @@
     return jnp.where((iota(head.shape, 1) == 0) & jnp.logical_not(live), MARK, head)
 
 
-def state_kernel(emb_ref, moves_ref, out_ref):
-    rows = emb_ref.shape[0]
-    values = emb_ref[...]
-    count = jnp.sum((moves_ref[0:1, :] >= 0).astype(f32), axis=1, keepdims=True)
-    live = iota((rows, 1), 0).astype(f32) < count
+def unit_rows(values, targets):
+    count = jnp.sum((targets >= 0).astype(f32), axis=1, keepdims=True)
+    live = iota((values.shape[0], 1), 0).astype(f32) < count
     total = jnp.sum(values * values, axis=1, keepdims=True)
-    unit = jnp.where(live, values * lax.rsqrt(total + epsilon), 0.0)
-    out_ref[:, LANES:] = unit[:, LANES:].astype(bf16)
-    out_ref[:, :LANES] = mark_empty(unit[:, :LANES], live).astype(bf16)
-
-
-def places_kernel(clusters, most, own_ref, peer_ref, out_ref):
+    unit = jnp.where(live, values * lax.rsqrt(total + epsilon), 0.0).astype(bf16)
+    flags = jnp.broadcast_to(live.astype(f32), (values.shape[0], LANES)).astype(bf16)
+    return unit, flags
+
+
+def state_kernel(emb_ref, moves_ref, out_ref, flags_ref):
+    out_ref[...], flags_ref[...] = unit_rows(emb_ref[...], moves_ref[0:1, :])
+
+
+def index_kernel(clusters, most, own_ref, peer_ref, wanted_ref, ahead_ref):
     lists, rows = own_ref.shape
     cluster, core = here()
     before = (iota((rows, rows), 0) < iota((rows, rows), 1)).astype(bf16)
@@ -62,44 +64,51 @@
             step = back >> 1
             mine = ((back & 1) ^ (step & 1)) == core
             place = (step * SHARES + (core ^ half)) * most + rank
-            out_ref[number : number + 1, half * rows : (half + 1) * rows] = jnp.where(
-                (targets >= 0) & mine, place, -1
-            )
+            place = jnp.where((targets >= 0) & mine, place, -1)
+            wanted_ref[number, :, half * rows : (half + 1) * rows] = (
+                iota((rows, rows), 0) == place
+            ).astype(bf16)
+    _, key = arrival(clusters, most, rows, iota((SHARES * rows, 1), 0))
+    _, other = arrival(clusters, most, rows, iota((1, SHARES * rows), 1))
+    ahead = key - other
+    ahead_ref[...] = ((ahead > 0) & (ahead < 2 * rows)).astype(bf16)
+
+
+def arrival(clusters, most, rows, index):
+    cluster, core = here()
+    half = (index >= rows).astype(i32)
+    inner = index - half * rows
+    step = inner // (SHARES * most)
+    share = (inner // most) & 1
+    source = cluster ^ offset_of(clusters, step, core ^ half)
+    return share, share * (4 * rows) + source * most + inner % most
 
 
 def pass_kernel(clusters, most, number, last, count, *refs):
-    blocks, (places_ref, *outs) = refs[:count], refs[count:]
+    blocks, outs = refs[:count], refs[count + 2 :]
+    wanted_ref, ahead_ref = refs[count : count + 2]
     width = blocks[0].shape[1]
-    total_rows = count * blocks[0].shape[0]
+    total_rows = ahead_ref.shape[0]
     rows = total_rows // SHARES
-    block = SHARES * most
-    cluster, core = here()
-
-    heads = jnp.concatenate([ref[:, :LANES] for ref in blocks], axis=0).astype(f32)
-    live = jnp.broadcast_to((heads[:, 0:1] < 1.5).astype(f32), (total_rows, LANES))
-    heads = jnp.where(live > 0.5, heads, 0.0).astype(bf16)
-    tails = jnp.concatenate([ref[:, LANES:] for ref in blocks], axis=0)
-    keys = jnp.concatenate([heads, tails], axis=1)
-    flags = live.astype(bf16)
 
     if number == 0:
-        place = places_ref[number : number + 1, :]
-        select = (iota((rows, total_rows), 0) == place).astype(bf16)
+        state_ref, flags_ref, peer_ref, targets_ref = blocks
+        peer, peer_flags = unit_rows(peer_ref[...], targets_ref[0:1, :])
+        keys = jnp.concatenate([state_ref[...], peer], axis=0)
+        flags = jnp.concatenate([flags_ref[...], peer_flags], axis=0)
+        scores = lax.dot_general(keys, keys, (((1,), (1,)), ((), ())), preferred_element_type=f32)
+        select = wanted_ref[number]
     else:
-
-        def order(index):
-            half = (index >= rows).astype(i32)
-            inner = index - half * rows
-            step = inner // block
-            share = (inner // most) & 1
-            source = cluster ^ offset_of(clusters, step, core ^ half)
-            return share, share * (4 * rows) + source * most + inner % most
-
-        share, key = order(iota((total_rows, 1), 0))
-        _, other = order(iota((1, total_rows), 1))
-        ahead = key - other
-        ahead = ((ahead > 0) & (ahead < 2 * rows)).astype(bf16)
-        slot = jnp.dot(ahead, flags, preferred_element_type=f32)
+        heads = jnp.concatenate([ref[:, :LANES] for ref in blocks], axis=0).astype(f32)
+        live = jnp.broadcast_to((heads[:, 0:1] < 1.5).astype(f32), (total_rows, LANES))
+        heads = jnp.where(live > 0.5, heads, 0.0).astype(bf16)
+        tails = jnp.concatenate([ref[:, LANES:] for ref in blocks], axis=0)
+        keys = jnp.concatenate([heads, tails], axis=1)
+        flags = live.astype(bf16)
+        scores = lax.dot_general(keys, keys, (((1,), (1,)), ((), ())), preferred_element_type=f32)
+        _, core = here()
+        share, _ = arrival(clusters, most, rows, iota((total_rows, 1), 0))
+        slot = jnp.dot(ahead_ref[...], flags, preferred_element_type=f32)
         slot = jnp.where(live > 0.5, slot, -1.0)[:, 0:1]
         lane = iota((total_rows, rows), 1).astype(f32)
         own = (share == core).astype(f32)
@@ -109,13 +118,11 @@
         else:
             theirs = ((slot == lane) & (own < 0.5)).astype(bf16)
             mine = jnp.concatenate([mine, theirs], axis=1)
-            place = places_ref[number : number + 1, :]
-            wanted = (iota((rows, total_rows), 0) == place).astype(bf16)
+            wanted = wanted_ref[number]
         select = lax.dot_general(
             wanted, mine, (((1,), (1,)), ((), ())), preferred_element_type=f32
         ).astype(bf16)
 
-    scores = lax.dot_general(keys, keys, (((1,), (1,)), ((), ())), preferred_element_type=f32)
     weights = jnp.exp(sharpness * (scores - 1.0)).astype(bf16)
     chosen = jnp.dot(select, weights, preferred_element_type=f32).astype(bf16)
     sums = jnp.dot(
@@ -171,17 +178,28 @@
     block = SHARES * most
     aligned = block % 16 == 0
     targets = moves[:, 0, 0, :]
+    values = embeddings[0, 0]
     peer_targets = swap_pair(targets)
-    state = call(
-        state_kernel, jax.ShapeDtypeStruct((rows, width), bf16), embeddings[0, 0], targets
-    )
-    places = call(
-        lambda *refs: places_kernel(clusters, most, *refs),
-        jax.ShapeDtypeStruct((targets.shape[0], SHARES * rows), i32),
+    peer_values = swap_pair(values)
+    state, flags = call(
+        state_kernel,
+        [
+            jax.ShapeDtypeStruct((rows, width), bf16),
+            jax.ShapeDtypeStruct((rows, LANES), bf16),
+        ],
+        values,
+        targets,
+    )
+    tables = call(
+        lambda *refs: index_kernel(clusters, most, *refs),
+        [
+            jax.ShapeDtypeStruct((targets.shape[0], rows, SHARES * rows), bf16),
+            jax.ShapeDtypeStruct((SHARES * rows, SHARES * rows), bf16),
+        ],
         targets,
         peer_targets,
     )
-    keys = [state, swap_pair(state)]
+    keys = [state, flags, peer_values, peer_targets]
     for number in range(PASSES):
         last = number + 1 == PASSES
         if last:
@@ -194,7 +212,7 @@
             lambda *refs: pass_kernel(clusters, most, number, last, len(keys), *refs),
             out,
             *keys,
-            places,
+            *tables,
         )
         if last:
             return result[None, None]

time: 34.1 us -> 32.9 us (0.965)
  waiting for transfers between devices: 12 us -> 11 us
  local copies, waits for them, and re-layouts: 1.74 us -> 1.25 us
    ppermute x10, waiting for transfers between devices: 3.04 us -> 1.98 us  [swap_pair(): return lax.ppermute(values, 'pair', [(0, 1), (1, 0)])]
    unnamed x4, local copies, waits for them, and re-layouts: 1.74 us -> 1.25 us
  transfers between devices with their start and end apart: 18 -> 18, of which waited for: 11 -> 10; matrix products, arithmetic and copies ran while one was open for 0% -> 0% of each run, Pallas kernels for 0% -> 1%
where the time goes in v4:
time: 32.9 us; the launch traced here: 32.7 us
  starting transfers between devices  15.4 us (47%)
  waiting for transfers between devices  11 us (33%)
  Pallas kernels  4.95 us (15%)
  local copies, waits for them, and re-layouts  1.25 us (4%)
    ppermute x8, starting transfers between devices, send(): return lax.ppermute(values, ('owner', 'sub', 'pair'), pairs)  13.1 us
    ppermute x8, waiting for transfers between devices, send(): return lax.ppermute(values, ('owner', 'sub', 'pair'), pairs)  9.05 us
    pallas_call x5, Pallas kernels, call(): pl.pallas_call(kernel, out_shape=out, in_specs=[spec] * len(args), out_sp...  4.95 us
    ppermute x10, starting transfers between devices, swap_pair(): return lax.ppermute(values, 'pair', [(0, 1), (1, 0)])  2.23 us
    ppermute x10, waiting for transfers between devices, swap_pair(): return lax.ppermute(values, 'pair', [(0, 1), (1, 0)])  1.98 us
    unnamed x4, local copies, waits for them, and re-layouts  1.25 us
  transfers between devices with their start and end apart: 18, of which 10 were waited for; matrix products, arithmetic and copies ran while one was open for 0% of the time, Pallas kernels for 1%

profile of v4, /device:TPU:0, one launch (start us, length us, event | category | flops | bytes accessed | tf_op | source)
XLA Modules:
  0.0 32.7 jit_solution(17199320521862483274)
XLA Ops:
  0.0 0.0 copy-start.1
  0.0 0.5 %collective-permute-start = (f32[128,1152]{1,0:T(8,128)}, f32[128,1152]{1,0:T(8,128)S(1)}, u32[]{:S(2)}, u32[]{:S(2)}) collective-permute-start(f32[128,1152]{1,0:T(8,128)} %bitcast.3), channel_id=1, source_target_pairs={{0,1},{1,0},{2,3},{3,2},{4,5},{5,4},{6,7},{7,6},{8,9},{9,8},{10,11... | collective-permute-start | bytes 1769480 | tf_op jit(solution)/shard_map/ppermute | solution.py:161
  0.5 0.2 copy-done.1
  0.7 0.5 %collective-permute-start.1 = (s32[2,128]{1,0:T(2,128)S(1)}, s32[2,128]{1,0:T(2,128)S(1)}, u32[]{:S(2)}, u32[]{:S(2)}) collective-permute-start(s32[2,128]{1,0:T(2,128)S(1)} %bitcast.5), channel_id=1, source_target_pairs={{0,1},{1,0},{2,3},{3,2},{4,5},{5,4},{6,7},{7,6},{8,9},{9,8},{10,11... | collective-permute-start | bytes 3080 | tf_op jit(solution)/shard_map/ppermute | solution.py:161
  1.2 0.0 copy-start
  1.2 1.1 %copy-done = f32[1,1,128,1152]{3,2,1,0:T(8,128)S(1)} copy-done((f32[1,1,128,1152]{3,2,1,0:T(8,128)S(1)}, f32[1,1,128,1152]{3,2,1,0:T(8,128)}, u32[]{:S(2)}) %copy-start) | copy-done | bytes 589848
  2.2 0.2 shard_map.28
  2.4 0.0 collective-permute-done.1.refs_1_.refs_3_
  2.4 0.3 shard_map.29
  2.7 0.0 collective-permute-done.refs_2_
  2.7 1.2 %shard_map.30 = (bf16[32,1152]{1,0:T(8,128)(2,1)S(1)}, bf16[32,1152]{1,0:T(8,128)(2,1)S(1)}, bf16[32,1152]{1,0:T(8,128)(2,1)S(1)}, bf16[32,1152]{1,0:T(8,128)(2,1)S(1)}) custom-call(bf16[128,1152]{1,0:T(8,128)(2,1)S(1)} %get-tuple-element.17.refs_0_, bf16[128,128]{1,0:T(8,128)(2,1)S(1)} %get-tuple-element.18.refs_1_, ...), custom_call_target="tpu_custom_call" | custom-call | tf_op jit(solution)/shard_map/pallas_call | solution.py:151
  3.9 5.9 %collective-permute-start.2 = (bf16[32,1152]{1,0:T(8,128)(2,1)S(1)}, bf16[32,1152]{1,0:T(8,128)(2,1)S(1)}, u32[]{:S(2)}, u32[]{:S(2)}) collective-permute-start(bf16[32,1152]{1,0:T(8,128)(2,1)S(1)} %get-tuple-element.21), channel_id=1, source_target_pairs={{0,14},{1,13},{2,12},{3,15},{4,10},{5,9},{6,8},{7,11},{8,6},{9,5},... | collective-permute-start | bytes 221192 | tf_op jit(solution)/shard_map/ppermute | solution.py:170
  9.8 0.0 collective-permute-start.3
  9.8 0.6 %collective-permute-start.4 = (bf16[32,1152]{1,0:T(8,128)(2,1)S(1)}, bf16[32,1152]{1,0:T(8,128)(2,1)S(1)}, u32[]{:S(2)}, u32[]{:S(2)}) collective-permute-start(bf16[32,1152]{1,0:T(8,128)(2,1)S(1)} %get-tuple-element.23), channel_id=1, source_target_pairs={{0,6},{1,5},{2,4},{3,7},{4,2},{5,1},{6,0},{7,3},{8,14},{9,13},{10,... | collective-permute-start | bytes 221192 | tf_op jit(solution)/shard_map/ppermute | solution.py:170
  10.4 0.7 %collective-permute-start.5 = (bf16[32,1152]{1,0:T(8,128)(2,1)S(1)}, bf16[32,1152]{1,0:T(8,128)(2,1)S(1)}, u32[]{:S(2)}, u32[]{:S(2)}) collective-permute-start(bf16[32,1152]{1,0:T(8,128)(2,1)S(1)} %get-tuple-element.24), channel_id=1, source_target_pairs={{0,0},{1,3},{2,2},{3,1},{4,4},{5,7},{6,6},{7,5},{8,8},{9,11},{10,1... | collective-permute-start | bytes 221192 | tf_op jit(solution)/shard_map/ppermute | solution.py:170
  11.1 1.8 %collective-permute-done.2.refs_0_ = bf16[32,1152]{1,0:T(8,128)(2,1)S(1)} collective-permute-done((bf16[32,1152]{1,0:T(8,128)(2,1)S(1)}, bf16[32,1152]{1,0:T(8,128)(2,1)S(1)}, u32[]{:S(2)}, u32[]{:S(2)}) %collective-permute-start.2) | collective-permute-done | bytes 73760 | tf_op jit(solution)/shard_map/ppermute | solution.py:170
  12.8 0.0 collective-permute-start.6
  12.9 2.8 %collective-permute-done.3.refs_1_ = bf16[32,1152]{1,0:T(8,128)(2,1)S(1)} collective-permute-done((bf16[32,1152]{1,0:T(8,128)(2,1)S(1)}, bf16[32,1152]{1,0:T(8,128)(2,1)S(1)}, u32[]{:S(2)}, u32[]{:S(2)}) %collective-permute-start.3) | collective-permute-done | bytes 73760 | tf_op jit(solution)/shard_map/ppermute | solution.py:170
  15.6 0.0 collective-permute-start.7
  15.6 0.9 %collective-permute-done.4.refs_2_ = bf16[32,1152]{1,0:T(8,128)(2,1)S(1)} collective-permute-done((bf16[32,1152]{1,0:T(8,128)(2,1)S(1)}, bf16[32,1152]{1,0:T(8,128)(2,1)S(1)}, u32[]{:S(2)}, u32[]{:S(2)}) %collective-permute-start.4) | collective-permute-done | bytes 73760 | tf_op jit(solution)/shard_map/ppermute | solution.py:170
  16.6 0.0 collective-permute-start.8
  16.6 0.0 collective-permute-done.5.refs_3_
  16.6 0.5 %collective-permute-start.9 = (bf16[32,1152]{1,0:T(8,128)(2,1)S(1)}, bf16[32,1152]{1,0:T(8,128)(2,1)S(1)}, u32[]{:S(2)}, u32[]{:S(2)}) collective-permute-start(bf16[32,1152]{1,0:T(8,128)(2,1)S(1)} %collective-permute-done.5.refs_3_), channel_id=1, source_target_pairs={{0,1},{1,0},{2,3},{3,2},{4,5},{5,4},{6,7},{7,6},{8,9},{9,8},{10,11... | collective-permute-start | bytes 221192 | tf_op jit(solution)/shard_map/ppermute | solution.py:161
  17.1 0.0 collective-permute-done.6.refs_4_
  17.1 0.0 collective-permute-done.7.refs_5_
  17.1 0.7 %collective-permute-done.8.refs_6_ = bf16[32,1152]{1,0:T(8,128)(2,1)S(1)} collective-permute-done((bf16[32,1152]{1,0:T(8,128)(2,1)S(1)}, bf16[32,1152]{1,0:T(8,128)(2,1)S(1)}, u32[]{:S(2)}, u32[]{:S(2)}) %collective-permute-start.8) | collective-permute-done | bytes 73760 | tf_op jit(solution)/shard_map/ppermute | solution.py:161
  17.8 0.2 collective-permute-done.9.refs_7_
  18.0 1.3 %shard_map.31 = (bf16[32,1152]{1,0:T(8,128)(2,1)S(1)}, bf16[32,1152]{1,0:T(8,128)(2,1)S(1)}, bf16[32,1152]{1,0:T(8,128)(2,1)S(1)}, bf16[32,1152]{1,0:T(8,128)(2,1)S(1)}) custom-call(bf16[32,1152]{1,0:T(8,128)(2,1)S(1)} %collective-permute-done.2.refs_0_, bf16[32,1152]{1,0:T(8,128)(2,1)S(1)} %collective-permute-done.3.refs_1_, ...), custom_call_target="tpu_custom_call" | custom-call | tf_op jit(solution)/shard_map/pallas_call | solution.py:151
  19.3 2.7 %collective-permute-start.10 = (bf16[32,1152]{1,0:T(8,128)(2,1)S(1)}, bf16[32,1152]{1,0:T(8,128)(2,1)S(1)}, u32[]{:S(2)}, u32[]{:S(2)}) collective-permute-start(bf16[32,1152]{1,0:T(8,128)(2,1)S(1)} %get-tuple-element.25), channel_id=1, source_target_pairs={{0,14},{1,13},{2,12},{3,15},{4,10},{5,9},{6,8},{7,11},{8,6},{9,5},... | collective-permute-start | bytes 221192 | tf_op jit(solution)/shard_map/ppermute | solution.py:170
  22.0 0.0 collective-permute-start.11
  22.0 2.7 %collective-permute-start.12 = (bf16[32,1152]{1,0:T(8,128)(2,1)S(1)}, bf16[32,1152]{1,0:T(8,128)(2,1)S(1)}, u32[]{:S(2)}, u32[]{:S(2)}) collective-permute-start(bf16[32,1152]{1,0:T(8,128)(2,1)S(1)} %get-tuple-element.27), channel_id=1, source_target_pairs={{0,6},{1,5},{2,4},{3,7},{4,2},{5,1},{6,0},{7,3},{8,14},{9,13},{10,... | collective-permute-start | bytes 221192 | tf_op jit(solution)/shard_map/ppermute | solution.py:170
  24.7 0.7 %collective-permute-start.13 = (bf16[32,1152]{1,0:T(8,128)(2,1)S(1)}, bf16[32,1152]{1,0:T(8,128)(2,1)S(1)}, u32[]{:S(2)}, u32[]{:S(2)}) collective-permute-start(bf16[32,1152]{1,0:T(8,128)(2,1)S(1)} %get-tuple-element.28), channel_id=1, source_target_pairs={{0,0},{1,3},{2,2},{3,1},{4,4},{5,7},{6,6},{7,5},{8,8},{9,11},{10,1... | collective-permute-start | bytes 221192 | tf_op jit(solution)/shard_map/ppermute | solution.py:170
  25.3 1.7 %collective-permute-done.10.refs_0_ = bf16[32,1152]{1,0:T(8,128)(2,1)S(1)} collective-permute-done((bf16[32,1152]{1,0:T(8,128)(2,1)S(1)}, bf16[32,1152]{1,0:T(8,128)(2,1)S(1)}, u32[]{:S(2)}, u32[]{:S(2)}) %collective-permute-start.10) | collective-permute-done | bytes 73760 | tf_op jit(solution)/shard_map/ppermute | solution.py:170
  27.0 0.0 collective-permute-start.14
  27.0 1.9 %collective-permute-done.11.refs_1_ = bf16[32,1152]{1,0:T(8,128)(2,1)S(1)} collective-permute-done((bf16[32,1152]{1,0:T(8,128)(2,1)S(1)}, bf16[32,1152]{1,0:T(8,128)(2,1)S(1)}, u32[]{:S(2)}, u32[]{:S(2)}) %collective-permute-start.11) | collective-permute-done | bytes 73760 | tf_op jit(solution)/shard_map/ppermute | solution.py:170
  28.9 0.2 collective-permute-start.15
  29.1 0.0 collective-permute-done.12.refs_2_
  29.1 0.3 collective-permute-start.16
  29.4 0.0 collective-permute-done.13.refs_3_
  29.4 0.2 collective-permute-start.17
  29.6 0.0 collective-permute-done.14.refs_4_
  29.6 0.5 %collective-permute-done.15.refs_5_ = bf16[32,1152]{1,0:T(8,128)(2,1)S(1)} collective-permute-done((bf16[32,1152]{1,0:T(8,128)(2,1)S(1)}, bf16[32,1152]{1,0:T(8,128)(2,1)S(1)}, u32[]{:S(2)}, u32[]{:S(2)}) %collective-permute-start.15) | collective-permute-done | bytes 73760 | tf_op jit(solution)/shard_map/ppermute | solution.py:161
  30.2 0.2 collective-permute-done.16.refs_6_
  30.4 0.3 collective-permute-done.17.refs_7_
  30.7 2.0 %shard_map.32 = f32[128,1152]{1,0:T(8,128)} custom-call(bf16[32,1152]{1,0:T(8,128)(2,1)S(1)} %collective-permute-done.10.refs_0_, bf16[32,1152]{1,0:T(8,128)(2,1)S(1)} %collective-permute-done.11.refs_1_, bf16[32,1152]{1,0:T(8,128)(2,1)S(1)} %collective-permute-done.12.refs_2_, bf16[32,1152]{1,0:T(8,128)(2,1)S(1)} %collective-permute-done.13.refs_3_, ...), custom_call_target="tpu_custom_call" | custom-call | tf_op jit(solution)/shard_map/pallas_call | solution.py:151
Async XLA Ops:
  0.0 0.7 %copy-start.1 = (s32[2,1,1,128]{3,2,1,0:T(1,128)S(1)}, s32[2,1,1,128]{3,2,1,0:T(1,128)}, u32[]{:S(2)}) copy-start(s32[2,1,1,128]{3,2,1,0:T(1,128)} %param.3) | copy-start | bytes 3076
  0.0 2.7 %collective-permute-start = (f32[128,1152]{1,0:T(8,128)}, f32[128,1152]{1,0:T(8,128)S(1)}, u32[]{:S(2)}, u32[]{:S(2)}) collective-permute-start(f32[128,1152]{1,0:T(8,128)} %bitcast.3), channel_id=1, source_target_pairs={{0,1},{1,0},{2,3},{3,2},{4,5},{5,4},{6,7},{7,6},{8,9},{9,8},{10,11... | collective-permute-start | bytes 1769480 | tf_op jit(solution)/shard_map/ppermute | solution.py:161
  0.7 1.7 %collective-permute-start.1 = (s32[2,128]{1,0:T(2,128)S(1)}, s32[2,128]{1,0:T(2,128)S(1)}, u32[]{:S(2)}, u32[]{:S(2)}) collective-permute-start(s32[2,128]{1,0:T(2,128)S(1)} %bitcast.5), channel_id=1, source_target_pairs={{0,1},{1,0},{2,3},{3,2},{4,5},{5,4},{6,7},{7,6},{8,9},{9,8},{10,11... | collective-permute-start | bytes 3080 | tf_op jit(solution)/shard_map/ppermute | solution.py:161
  1.2 1.1 %copy-start = (f32[1,1,128,1152]{3,2,1,0:T(8,128)S(1)}, f32[1,1,128,1152]{3,2,1,0:T(8,128)}, u32[]{:S(2)}) copy-start(f32[1,1,128,1152]{3,2,1,0:T(8,128)} %param.2) | copy-start | bytes 1769476
  3.9 8.9 %collective-permute-start.2 = (bf16[32,1152]{1,0:T(8,128)(2,1)S(1)}, bf16[32,1152]{1,0:T(8,128)(2,1)S(1)}, u32[]{:S(2)}, u32[]{:S(2)}) collective-permute-start(bf16[32,1152]{1,0:T(8,128)(2,1)S(1)} %get-tuple-element.21), channel_id=1, source_target_pairs={{0,14},{1,13},{2,12},{3,15},{4,10},{5,9},{6,8},{7,11},{8,6},{9,5},... | collective-permute-start | bytes 221192 | tf_op jit(solution)/shard_map/ppermute | solution.py:170
  9.8 5.8 %collective-permute-start.3 = (bf16[32,1152]{1,0:T(8,128)(2,1)S(1)}, bf16[32,1152]{1,0:T(8,128)(2,1)S(1)}, u32[]{:S(2)}, u32[]{:S(2)}) collective-permute-start(bf16[32,1152]{1,0:T(8,128)(2,1)S(1)} %get-tuple-element.22), channel_id=1, source_target_pairs={{0,8},{1,11},{2,10},{3,9},{4,12},{5,15},{6,14},{7,13},{8,0},{9,3},... | collective-permute-start | bytes 221192 | tf_op jit(solution)/shard_map/ppermute | solution.py:170
  9.8 6.8 %collective-permute-start.4 = (bf16[32,1152]{1,0:T(8,128)(2,1)S(1)}, bf16[32,1152]{1,0:T(8,128)(2,1)S(1)}, u32[]{:S(2)}, u32[]{:S(2)}) collective-permute-start(bf16[32,1152]{1,0:T(8,128)(2,1)S(1)} %get-tuple-element.23), channel_id=1, source_target_pairs={{0,6},{1,5},{2,4},{3,7},{4,2},{5,1},{6,0},{7,3},{8,14},{9,13},{10,... | collective-permute-start | bytes 221192 | tf_op jit(solution)/shard_map/ppermute | solution.py:170
  10.4 6.1 %collective-permute-start.5 = (bf16[32,1152]{1,0:T(8,128)(2,1)S(1)}, bf16[32,1152]{1,0:T(8,128)(2,1)S(1)}, u32[]{:S(2)}, u32[]{:S(2)}) collective-permute-start(bf16[32,1152]{1,0:T(8,128)(2,1)S(1)} %get-tuple-element.24), channel_id=1, source_target_pairs={{0,0},{1,3},{2,2},{3,1},{4,4},{5,7},{6,6},{7,5},{8,8},{9,11},{10,1... | collective-permute-start | bytes 221192 | tf_op jit(solution)/shard_map/ppermute | solution.py:170
  12.8 4.2 %collective-permute-start.6 = (bf16[32,1152]{1,0:T(8,128)(2,1)S(1)}, bf16[32,1152]{1,0:T(8,128)(2,1)S(1)}, u32[]{:S(2)}, u32[]{:S(2)}) collective-permute-start(bf16[32,1152]{1,0:T(8,128)(2,1)S(1)} %collective-permute-done.2.refs_0_), channel_id=1, source_target_pairs={{0,1},{1,0},{2,3},{3,2},{4,5},{5,4},{6,7},{7,6},{8,9},{9,8},{10,11... | collective-permute-start | bytes 221192 | tf_op jit(solution)/shard_map/ppermute | solution.py:161
  15.6 1.5 %collective-permute-start.7 = (bf16[32,1152]{1,0:T(8,128)(2,1)S(1)}, bf16[32,1152]{1,0:T(8,128)(2,1)S(1)}, u32[]{:S(2)}, u32[]{:S(2)}) collective-permute-start(bf16[32,1152]{1,0:T(8,128)(2,1)S(1)} %collective-permute-done.3.refs_1_), channel_id=1, source_target_pairs={{0,1},{1,0},{2,3},{3,2},{4,5},{5,4},{6,7},{7,6},{8,9},{9,8},{10,11... | collective-permute-start | bytes 221192 | tf_op jit(solution)/shard_map/ppermute | solution.py:161
  16.6 1.3 %collective-permute-start.8 = (bf16[32,1152]{1,0:T(8,128)(2,1)S(1)}, bf16[32,1152]{1,0:T(8,128)(2,1)S(1)}, u32[]{:S(2)}, u32[]{:S(2)}) collective-permute-start(bf16[32,1152]{1,0:T(8,128)(2,1)S(1)} %collective-permute-done.4.refs_2_), channel_id=1, source_target_pairs={{0,1},{1,0},{2,3},{3,2},{4,5},{5,4},{6,7},{7,6},{8,9},{9,8},{10,11... | collective-permute-start | bytes 221192 | tf_op jit(solution)/shard_map/ppermute | solution.py:161
  16.6 1.4 %collective-permute-start.9 = (bf16[32,1152]{1,0:T(8,128)(2,1)S(1)}, bf16[32,1152]{1,0:T(8,128)(2,1)S(1)}, u32[]{:S(2)}, u32[]{:S(2)}) collective-permute-start(bf16[32,1152]{1,0:T(8,128)(2,1)S(1)} %collective-permute-done.5.refs_3_), channel_id=1, source_target_pairs={{0,1},{1,0},{2,3},{3,2},{4,5},{5,4},{6,7},{7,6},{8,9},{9,8},{10,11... | collective-permute-start | bytes 221192 | tf_op jit(solution)/shard_map/ppermute | solution.py:161
  19.3 7.7 %collective-permute-start.10 = (bf16[32,1152]{1,0:T(8,128)(2,1)S(1)}, bf16[32,1152]{1,0:T(8,128)(2,1)S(1)}, u32[]{:S(2)}, u32[]{:S(2)}) collective-permute-start(bf16[32,1152]{1,0:T(8,128)(2,1)S(1)} %get-tuple-element.25), channel_id=1, source_target_pairs={{0,14},{1,13},{2,12},{3,15},{4,10},{5,9},{6,8},{7,11},{8,6},{9,5},... | collective-permute-start | bytes 221192 | tf_op jit(solution)/shard_map/ppermute | solution.py:170
  22.0 6.9 %collective-permute-start.11 = (bf16[32,1152]{1,0:T(8,128)(2,1)S(1)}, bf16[32,1152]{1,0:T(8,128)(2,1)S(1)}, u32[]{:S(2)}, u32[]{:S(2)}) collective-permute-start(bf16[32,1152]{1,0:T(8,128)(2,1)S(1)} %get-tuple-element.26), channel_id=1, source_target_pairs={{0,8},{1,11},{2,10},{3,9},{4,12},{5,15},{6,14},{7,13},{8,0},{9,3},... | collective-permute-start | bytes 221192 | tf_op jit(solution)/shard_map/ppermute | solution.py:170
  22.0 7.1 %collective-permute-start.12 = (bf16[32,1152]{1,0:T(8,128)(2,1)S(1)}, bf16[32,1152]{1,0:T(8,128)(2,1)S(1)}, u32[]{:S(2)}, u32[]{:S(2)}) collective-permute-start(bf16[32,1152]{1,0:T(8,128)(2,1)S(1)} %get-tuple-element.27), channel_id=1, source_target_pairs={{0,6},{1,5},{2,4},{3,7},{4,2},{5,1},{6,0},{7,3},{8,14},{9,13},{10,... | collective-permute-start | bytes 221192 | tf_op jit(solution)/shard_map/ppermute | solution.py:170
  24.7 4.8 %collective-permute-start.13 = (bf16[32,1152]{1,0:T(8,128)(2,1)S(1)}, bf16[32,1152]{1,0:T(8,128)(2,1)S(1)}, u32[]{:S(2)}, u32[]{:S(2)}) collective-permute-start(bf16[32,1152]{1,0:T(8,128)(2,1)S(1)} %get-tuple-element.28), channel_id=1, source_target_pairs={{0,0},{1,3},{2,2},{3,1},{4,4},{5,7},{6,6},{7,5},{8,8},{9,11},{10,1... | collective-permute-start | bytes 221192 | tf_op jit(solution)/shard_map/ppermute | solution.py:170
  27.0 2.6 %collective-permute-start.14 = (bf16[32,1152]{1,0:T(8,128)(2,1)S(1)}, bf16[32,1152]{1,0:T(8,128)(2,1)S(1)}, u32[]{:S(2)}, u32[]{:S(2)}) collective-permute-start(bf16[32,1152]{1,0:T(8,128)(2,1)S(1)} %collective-permute-done.10.refs_0_), channel_id=1, source_target_pairs={{0,1},{1,0},{2,3},{3,2},{4,5},{5,4},{6,7},{7,6},{8,9},{9,8},{10,11... | collective-permute-start | bytes 221192 | tf_op jit(solution)/shard_map/ppermute | solution.py:161
  28.9 1.3 %collective-permute-start.15 = (bf16[32,1152]{1,0:T(8,128)(2,1)S(1)}, bf16[32,1152]{1,0:T(8,128)(2,1)S(1)}, u32[]{:S(2)}, u32[]{:S(2)}) collective-permute-start(bf16[32,1152]{1,0:T(8,128)(2,1)S(1)} %collective-permute-done.11.refs_1_), channel_id=1, source_target_pairs={{0,1},{1,0},{2,3},{3,2},{4,5},{5,4},{6,7},{7,6},{8,9},{9,8},{10,11... | collective-permute-start | bytes 221192 | tf_op jit(solution)/shard_map/ppermute | solution.py:161
  29.1 1.3 %collective-permute-start.16 = (bf16[32,1152]{1,0:T(8,128)(2,1)S(1)}, bf16[32,1152]{1,0:T(8,128)(2,1)S(1)}, u32[]{:S(2)}, u32[]{:S(2)}) collective-permute-start(bf16[32,1152]{1,0:T(8,128)(2,1)S(1)} %collective-permute-done.12.refs_2_), channel_id=1, source_target_pairs={{0,1},{1,0},{2,3},{3,2},{4,5},{5,4},{6,7},{7,6},{8,9},{9,8},{10,11... | collective-permute-start | bytes 221192 | tf_op jit(solution)/shard_map/ppermute | solution.py:161
  29.4 1.3 %collective-permute-start.17 = (bf16[32,1152]{1,0:T(8,128)(2,1)S(1)}, bf16[32,1152]{1,0:T(8,128)(2,1)S(1)}, u32[]{:S(2)}, u32[]{:S(2)}) collective-permute-start(bf16[32,1152]{1,0:T(8,128)(2,1)S(1)} %collective-permute-done.13.refs_3_), channel_id=1, source_target_pairs={{0,1},{1,0},{2,3},{3,2},{4,5},{5,4},{6,7},{7,6},{8,9},{9,8},{10,11... | collective-permute-start | bytes 221192 | tf_op jit(solution)/shard_map/ppermute | solution.py:161
